TPU v7x, 128 devices: a whole 4x4x4 slice. The times are simulated.
128 devices in a mesh: rows: 4 (over x), cols: 32 (over y, z, core).
Axes of the slice: x: 4, y: 4, z: 4, core: 2. Of those that a mesh axis runs over, the one named last changes fastest.
Arguments:
- weight: bfloat16 [8192, 16384], P('rows', 'cols'), may hold values from -0.046875 to 0.046875
- hess_inv: float32 [16384, 16384], P('rows', 'cols'), as said below
- selected: int32 [3, 64], replicated, may hold values from 0 to 16383, as said below
- block_mask: int32 [8192, 128], P('rows'), may hold values 0 or 1
- row_limits: int32 [8192], P('rows'), may hold values from 16 to 128
- calibration: bfloat16 [1024, 16384], P(None, 'cols'), may hold values from -6 to 6
Outputs:
- pruned: bfloat16 [8192, 16384], P('rows', 'cols')
- layer_error: float32 [8192, 1024], P('rows', 'cols')
Inputs may be any that keep to these rules, and one draw needn't show every extreme that they name: `selected`: all 192 entries differ; 0 and 16383 are among them. `hess_inv`: symmetric positive definite.
All inputs are finite; a program needn't handle non-finite values. No bound on the sum of `block_mask` on one device may be relied on, other than what follows from the above.
Results may differ from a plain program's by a relative error of at most 0.005.
Values may be sent and summed in bfloat16 or wider, within the bound.
A program may use at most 128 MiB of HBM per device.

v0:
```python
import jax
import jax.numpy as jnp
from jax import lax
from jax.sharding import PartitionSpec as P

STEPS = 3
BLK = 128


def local(weight, hess_inv, selected, block_mask, row_limits, calibration):
    rows_local, cols_local = hess_inv.shape
    out_local = weight.shape[0]
    row_offset = lax.axis_index("rows") * rows_local
    col_offset = lax.axis_index("cols") * cols_local
    refit = weight.astype(jnp.float32)
    inverse = hess_inv
    for iteration in range(STEPS):
        chosen = selected[iteration]
        row_place = chosen - row_offset
        row_inside = (row_place >= 0) & (row_place < rows_local)
        row_pick = jnp.where(
            row_inside[:, None],
            jnp.take(inverse, jnp.clip(row_place, 0, rows_local - 1), axis=0),
            0.0,
        )
        panel = lax.psum(row_pick, "rows")
        col_place = chosen - col_offset
        col_inside = (col_place >= 0) & (col_place < cols_local)
        col_index = jnp.clip(col_place, 0, cols_local - 1)
        inverse_pick = jnp.where(col_inside[None, :], jnp.take(inverse, col_index, axis=1), 0.0)
        refit_pick = jnp.where(col_inside[None, :], jnp.take(refit, col_index, axis=1), 0.0)
        square_pick = jnp.where(col_inside[None, :], jnp.take(panel, col_index, axis=1), 0.0)
        inverse_cols, refit_cols, square = lax.psum((inverse_pick, refit_pick, square_pick), "cols")
        factor = jnp.linalg.cholesky(square)
        coeffs = jax.scipy.linalg.cho_solve((factor, True), panel)
        refit = refit - jnp.dot(refit_cols, coeffs, precision=lax.Precision.HIGHEST)
        inverse = inverse - jnp.dot(inverse_cols, coeffs, precision=lax.Precision.HIGHEST)
    blocks_local = cols_local // BLK
    running_count = jnp.cumsum(block_mask, axis=1)
    retained = block_mask * (running_count <= row_limits[:, None]).astype(jnp.int32)
    own_blocks = lax.dynamic_slice_in_dim(
        retained, lax.axis_index("cols") * blocks_local, blocks_local, 1
    )
    masked = (
        refit.reshape(out_local, blocks_local, BLK) * own_blocks.astype(jnp.float32)[:, :, None]
    ).reshape(out_local, cols_local)
    pruned = masked.astype(jnp.bfloat16)
    difference = (weight.astype(jnp.float32) - masked).astype(jnp.bfloat16)
    widened = lax.all_to_all(difference, "cols", split_axis=0, concat_axis=1, tiled=True)
    row_result = lax.dot_general(
        widened,
        lax.all_gather(calibration, "cols", axis=1, tiled=True),
        (((1,), (1,)), ((), ())),
        preferred_element_type=jnp.float32,
    )
    layer_error = lax.all_to_all(
        row_result.astype(jnp.bfloat16), "cols", split_axis=1, concat_axis=0, tiled=True
    ).astype(row_result.dtype)
    return (pruned, layer_error)


def solution(mesh):
    placed = (
        P("rows", "cols"),
        P("rows", "cols"),
        P(),
        P("rows", None),
        P("rows"),
        P(None, "cols"),
    )
    return jax.shard_map(
        local,
        mesh=mesh,
        in_specs=placed,
        out_specs=(P("rows", "cols"), P("rows", "cols")),
        check_vma=False,
    )
```

profile of v0, /device:TPU:1, one launch (start us, length us, event | category | flops | bytes accessed | tf_op | source)
XLA Modules:
  0.0 926.0 jit_solution(10366670984295173127)
XLA Ops:
  22.2 9.0 copy.60
  37.1 19.3 %all-reduce.11.cloned.1.call-done = f32[64,512]{1,0:T(8,128)} async-done(((f32[64,512]{1,0:T(8,128)}), f32[64,512]{1,0:T(8,128)}) %all-reduce.11.cloned.1.call-update) | async-done | bytes 131088 | tf_op jit(solution)/shard_map/psum | solution.py:26
  58.1 123.4 %psum.79 = f32[64,64]{0,1:T(8,128)S(1)} all-reduce(f32[64,64]{0,1:T(8,128)S(1)} %bitcast_select_fusion.7), channel_id=1, replica_groups=mesh['rows'=4,'cols'=32] {'cols'}, use_global_device_ids=true, to_apply=%region_2.6 | all-reduce | flops 4096 | bytes 32768 | tf_op jit(solution)/shard_map/psum | solution.py:33
  181.6 5.8 cholesky.59
  188.7 4.9 custom-call.9
  195.2 6.2 convolution_subtract_fusion.3
  201.4 5.4 copy.59
  211.2 107.3 %all-reduce.19.cloned.1.call-done = (f32[2048,64]{0,1:T(8,128)}, f32[4096,64]{0,1:T(8,128)}) async-done(((f32[2048,64]{0,1:T(8,128)}, f32[4096,64]{0,1:T(8,128)}), (f32[2048,64]{0,1:T(8,128)}, f32[4096,64]{0,1:T(8,128)})) %all-reduce.19.cloned.1.call-update) | async-done | bytes 1572880 | tf_op jit(solution)/shard_map/psum | solution.py:33
  318.4 11.5 %convolution_subtract_fusion.1 = f32[4096,512]{1,0:T(8,128)} fusion(f32[4096,512]{1,0:T(8,128)} %param.18, f32[4096,64]{0,1:T(8,128)} %get-tuple-element.10, f32[64,512]{1,0:T(8,128)S(1)} %fusion.14), kind=kOutput, calls=%fused_computation.12 | convolution fusion | flops 1612709888 | bytes 17956864 | tf_op jit(solution)/shard_map/dot_general | solution.py:37
  330.0 8.9 copy.64
  349.7 33.0 %all-reduce.13.cloned.1.call-done = f32[64,512]{1,0:T(8,128)} async-done(((f32[64,512]{1,0:T(8,128)}), f32[64,512]{1,0:T(8,128)}) %all-reduce.13.cloned.1.call-update) | async-done | bytes 131088 | tf_op jit(solution)/shard_map/psum | solution.py:26
  384.4 123.3 %psum.83 = f32[64,64]{0,1:T(8,128)S(1)} all-reduce(f32[64,64]{0,1:T(8,128)S(1)} %bitcast_select_fusion.6), channel_id=1, replica_groups=mesh['rows'=4,'cols'=32] {'cols'}, use_global_device_ids=true, to_apply=%region_8.15 | all-reduce | flops 4096 | bytes 32768 | tf_op jit(solution)/shard_map/psum | solution.py:33
  507.9 5.8 cholesky.70
  521.5 6.8 convolution_subtract_fusion.2
  528.2 5.4 copy.63
  538.1 107.4 %all-reduce.17.cloned.1.call-done = (f32[2048,64]{0,1:T(8,128)}, f32[4096,64]{0,1:T(8,128)}) async-done(((f32[2048,64]{0,1:T(8,128)}, f32[4096,64]{0,1:T(8,128)}), (f32[2048,64]{0,1:T(8,128)}, f32[4096,64]{0,1:T(8,128)})) %all-reduce.17.cloned.1.call-update) | async-done | bytes 1572880 | tf_op jit(solution)/shard_map/psum | solution.py:33
  645.4 11.5 %convolution_subtract_fusion = f32[4096,512]{1,0:T(8,128)} fusion(f32[4096,512]{1,0:T(8,128)} %convolution_subtract_fusion.1, f32[4096,64]{0,1:T(8,128)} %get-tuple-element.6, f32[64,512]{1,0:T(8,128)S(1)} %fusion.9), kind=kOutput, calls=%fused_computation.11 | convolution fusion | flops 1612709888 | bytes 17956864 | tf_op jit(solution)/shard_map/dot_general | solution.py:37
  667.2 33.6 %all-reduce.15.cloned.1.call-done = f32[64,512]{1,0:T(8,128)} async-done(((f32[64,512]{1,0:T(8,128)}), f32[64,512]{1,0:T(8,128)}) %all-reduce.15.cloned.1.call-update) | async-done | bytes 131088 | tf_op jit(solution)/shard_map/psum | solution.py:26
  702.6 127.2 %psum.87 = f32[64,64]{0,1:T(8,128)S(1)} all-reduce(f32[64,64]{0,1:T(8,128)S(1)} %bitcast_select_fusion.5), channel_id=1, replica_groups=mesh['rows'=4,'cols'=32] {'cols'}, use_global_device_ids=true, to_apply=%region_12.19 | all-reduce | flops 4096 | bytes 32768 | tf_op jit(solution)/shard_map/psum | solution.py:33
  829.8 5.8 cholesky.81
  848.3 5.5 subtract_convert_fusion
  853.8 36.5 %all_to_all.32 = bf16[32,64,512]{2,1,0:T(8,128)(2,1)S(1)} all-to-all(bf16[32,64,512]{2,1,0:T(8,128)(2,1)S(1)} %bitcast.115), channel_id=1, replica_groups=mesh['rows'=4,'cols'=32] {'cols'}, dimensions={0} | all-to-all | bytes 4194304 | tf_op jit(solution)/shard_map/all_to_all | solution.py:49
  890.5 15.4 %convolution_convert_fusion = bf16[64,1024]{1,0:T(8,128)(2,1)S(1)} fusion(bf16[64,16384]{1,0:T(8,128)(2,1)S(1)} %bitcast.113, bf16[1024,16384]{1,0:T(8,128)(2,1)} %all-gather.2.cloned.1.call-done), kind=kOutput, calls=%fused_computation.17 | convolution fusion | flops 2147549184 | bytes 35782656 | tf_op jit(solution)/shard_map/dot_general | solution.py:50
  906.3 11.4 %all_to_all.33 = bf16[32,2,1024]{2,1,0:T(2,128)(2,1)S(1)} all-to-all(bf16[32,2,1024]{2,1,0:T(2,128)(2,1)S(1)} %reshape.238), channel_id=1, replica_groups=mesh['rows'=4,'cols'=32] {'cols'}, dimensions={0} | all-to-all | bytes 262144 | tf_op jit(solution)/shard_map/all_to_all | solution.py:56
  (93 shorter events, 81.1 us)
Async XLA Ops:
  7.2 49.2 %all-reduce.11.cloned.1.call-start = ((), (), s32[]{:S(2)}) async-start(), calls=%async_computation.3 | async-start | bytes 262144 | tf_op jit(solution)/shard_map/psum | solution.py:26
  13.7 181.4 %all-reduce.9.cloned.1.call-start = ((), (), s32[]{:S(2)}) async-start(), calls=%async_computation.2 | async-start | bytes 1048576 | tf_op jit(solution)/shard_map/psum | solution.py:33
  22.1 296.3 %all-reduce.19.cloned.1.call-start = ((), (), s32[]{:S(2)}) async-start(), calls=%async_computation.8 | async-start | bytes 3145728 | tf_op jit(solution)/shard_map/psum | solution.py:33
  35.9 159.3 %copy-start.1 = (bf16[2048,512]{1,0:T(8,128)(2,1)S(1)}, bf16[2048,512]{1,0:T(8,128)(2,1)}, u32[]{:S(2)}) copy-start(bf16[2048,512]{1,0:T(8,128)(2,1)} %param.17) | copy-start | bytes 6291460
  210.9 171.8 %all-reduce.13.cloned.1.call-start = ((), (), s32[]{:S(2)}) async-start(), calls=%async_computation.4 | async-start | bytes 262144 | tf_op jit(solution)/shard_map/psum | solution.py:26
  343.8 301.7 %all-reduce.17.cloned.1.call-start = ((), (), s32[]{:S(2)}) async-start(), calls=%async_computation.7 | async-start | bytes 3145728 | tf_op jit(solution)/shard_map/psum | solution.py:33
  537.8 163.0 %all-reduce.15.cloned.1.call-start = ((), (), s32[]{:S(2)}) async-start(), calls=%async_computation.5 | async-start | bytes 262144 | tf_op jit(solution)/shard_map/psum | solution.py:26
  657.0 9.0 copy-start.3
  661.9 228.7 %all-gather.2.cloned.1.call-start = ((), (), s32[]{:S(2)}) async-start(), calls=%async_computation.6 | async-start | bytes 34603008 | tf_op jit(solution)/shard_map/all_gather | solution.py:52
  841.9 6.4 copy-start
  841.9 6.3 copy-start.2
Sparse Core Ops, SparseCore 0:
  13.8 42.4 all-reduce.10
  59.6 107.1 all-reduce.8
  211.0 107.3 all-reduce.18
  343.9 38.7 all-reduce.12
  537.9 107.4 all-reduce.16
  662.0 38.8 all-reduce.14
  703.0 128.8 all-gather.1
where the time goes:
time: 927 us; the launch traced here: 926 us
  blocking collectives  422 us (46%)
  waiting for transfers between devices  301 us (32%)
  local copies, waits for them, and re-layouts  77.9 us (8%)
  matrix products  61.5 us (7%)
  other arithmetic  48.2 us (5%)
  between operations  14.5 us (2%)
    psum x3, blocking collectives, local(): lax.psum((inverse_pick, refit_pick, square_pick), 'cols')  374 us
    psum x3, waiting for transfers between devices, local(): lax.psum((inverse_pick, refit_pick, square_pick), 'cols')  215 us
    psum x3, waiting for transfers between devices, local(): panel = lax.psum(row_pick, 'rows')  85.9 us
    all_to_all x1, blocking collectives, local(): lax.all_to_all(difference, 'cols', split_axis=0, concat_axis=1, tiled=True)  36.5 us
    dot_general x2, matrix products, local(): jnp.dot(inverse_cols, coeffs, precision=lax.Precision.HIGHEST)  23.1 us
    another operation x9, other arithmetic, local(): factor = jnp.linalg.cholesky(square)  19.6 us
  transfers between devices with their start and end apart: 7, of which 5 were waited for; matrix products, arithmetic and copies ran while one was open for 8% of the time, Pallas kernels for 0%

commit v1 on v0

v1 whole, which is shorter than its diff:
```python
import jax
import jax.numpy as jnp
from jax import lax
from jax.sharding import PartitionSpec as P

BLK = 128


def local(weight, hess_inv, selected, block_mask, row_limits, calibration):
    rows_local, cols_local = hess_inv.shape
    out_local = weight.shape[0]
    group = lax.axis_size("cols")
    row_offset = lax.axis_index("rows") * rows_local
    col_offset = lax.axis_index("cols") * cols_local
    chosen = selected.reshape(-1)
    row_place = chosen - row_offset
    row_inside = (row_place >= 0) & (row_place < rows_local)
    own_rows = jnp.where(
        row_inside[:, None],
        jnp.take(hess_inv, jnp.clip(row_place, 0, rows_local - 1), axis=0),
        0.0,
    )
    onehot = (
        lax.broadcasted_iota(jnp.int32, (cols_local, chosen.shape[0]), 0) == (chosen - col_offset)[None, :]
    )
    square = lax.psum(
        jnp.dot(own_rows, onehot.astype(jnp.float32), precision=lax.Precision.HIGHEST), ("rows", "cols")
    )
    panel = lax.psum(own_rows, "rows")
    weight_cols = lax.psum(
        jnp.dot(weight, onehot.astype(jnp.bfloat16), preferred_element_type=jnp.float32).astype(jnp.bfloat16), "cols"
    )
    factor = jnp.linalg.cholesky(square)
    coeffs = jax.scipy.linalg.cho_solve((factor, True), panel)
    wide = weight.astype(jnp.float32)
    refit = wide - jnp.dot(weight_cols.astype(jnp.float32), coeffs, precision=lax.Precision.HIGHEST)
    blocks_local = cols_local // BLK
    running_count = jnp.cumsum(block_mask, axis=1)
    retained = block_mask * (running_count <= row_limits[:, None]).astype(jnp.int32)
    own_blocks = lax.dynamic_slice_in_dim(
        retained, lax.axis_index("cols") * blocks_local, blocks_local, 1
    )
    masked = (
        refit.reshape(out_local, blocks_local, BLK) * own_blocks.astype(jnp.float32)[:, :, None]
    ).reshape(out_local, cols_local)
    pruned = masked.astype(jnp.bfloat16)
    difference = (wide - masked).astype(jnp.bfloat16)
    tokens = calibration.shape[0]
    partial = lax.dot_general(
        calibration.reshape(group, tokens // group, cols_local),
        difference,
        (((2,), (1,)), ((), ())),
        preferred_element_type=jnp.float32,
    ).astype(jnp.bfloat16)
    pieces = lax.all_to_all(partial, "cols", split_axis=0, concat_axis=0, tiled=True)
    layer_error = jnp.sum(pieces.astype(jnp.float32), axis=0).T
    return (pruned, layer_error)


def solution(mesh):
    placed = (
        P("rows", "cols"),
        P("rows", "cols"),
        P(),
        P("rows", None),
        P("rows"),
        P(None, "cols"),
    )
    return jax.shard_map(
        local,
        mesh=mesh,
        in_specs=placed,
        out_specs=(P("rows", "cols"), P("rows", "cols")),
        check_vma=False,
    )
```

time: 927 us -> 393 us (0.42)
  blocking collectives: 422 us -> 56.3 us
  waiting for transfers between devices: 301 us -> 225 us
  local copies, waits for them, and re-layouts: 77.9 us -> 16.4 us
  matrix products: 61.5 us -> 16.5 us
  other arithmetic: 48.2 us -> 61.9 us
    psum x3 -> x0, blocking collectives: 374 us -> none  [local(): lax.psum((inverse_pick, refit_pick, square_pick), 'cols')]
    psum x6 -> x3, waiting for transfers between devices: 301 us -> 225 us  [the longest x1 137 us: local(): lax.psum(jnp.dot(own_rows, onehot.astype(jnp.float32), precision=lax.Prec...]
    dot_general x6 -> x4, matrix products: 56.9 us -> 9.12 us  [the longest x1 3.69 us: local(): jnp.dot(weight_cols.astype(jnp.float32), coeffs, precision=lax.Precision....]
    gather x11 -> x1, local copies, waits for them, and re-layouts: 33.2 us -> 5.17 us  [local(): jnp.take(hess_inv, jnp.clip(row_place, 0, rows_local - 1), axis=0)]
    sub x3 -> x1, local copies, waits for them, and re-layouts: 19.7 us -> 0.08 us  [local(): chosen - col_offset]
    another operation x9 -> x7, other arithmetic: 19.6 us -> 30.1 us  [local(): factor = jnp.linalg.cholesky(square)]
    all_to_all x2 -> x1, blocking collectives: 47.9 us -> 56.3 us  [local(): lax.all_to_all(partial, 'cols', split_axis=0, concat_axis=0, tiled=True)]
  transfers between devices with their start and end apart: 7 -> 3, of which waited for: 5 -> 2; matrix products, arithmetic and copies ran while one was open for 8% -> 19% of each run, Pallas kernels for 0% -> 0%
where the time goes in v1:
time: 393 us; the launch traced here: 392 us
  waiting for transfers between devices  225 us (57%)
  other arithmetic  61.9 us (16%)
  blocking collectives  56.3 us (14%)
  matrix products  16.5 us (4%)
  local copies, waits for them, and re-layouts  16.4 us (4%)
  between operations  15.2 us (4%)
    psum x1, waiting for transfers between devices, local(): lax.psum(jnp.dot(own_rows, onehot.astype(jnp.float32), precision=lax.Prec...  137 us
    psum x1, waiting for transfers between devices, local(): lax.psum(jnp.dot(weight, onehot.astype(jnp.bfloat16), preferred_element_t...  87.9 us
    all_to_all x1, blocking collectives, local(): lax.all_to_all(partial, 'cols', split_axis=0, concat_axis=0, tiled=True)  56.3 us
    another operation x7, other arithmetic, local(): factor = jnp.linalg.cholesky(square)  30.1 us
    another operation x6, other arithmetic, local(): coeffs = jax.scipy.linalg.cho_solve((factor, True), panel)  22.7 us
  transfers between devices with their start and end apart: 3, of which 2 were waited for; matrix products, arithmetic and copies ran while one was open for 19% of the time, Pallas kernels for 0%

profile of v1, /device:TPU:1, one launch (start us, length us, event | category | flops | bytes accessed | tf_op | source)
XLA Modules:
  0.0 391.7 jit_solution(5587726836660570919)
XLA Ops:
  9.2 5.2 %gather_fusion = f32[192,512]{1,0:T(8,128)} fusion(f32[4096,512]{1,0:T(8,128)} %param.7, s32[1024]{0:T(1024)S(1)} %pad_clamp_fusion), kind=kCustom, calls=%fused_computation | custom fusion | bytes 787200 | tf_op jit(solution)/shard_map/jit(_take)/gather | solution.py:20
  14.3 1.1 select_select_fusion
  15.5 1.3 fusion.5
  17.6 1.8 fusion.2
  20.0 2.5 copy.10
  22.5 3.1 reduce_window_sum.11
  26.5 1.3 copy.12
  27.8 136.7 %all-reduce.9.cloned.1.call-done = f32[192,192]{0,1:T(8,128)} async-done(((f32[192,192]{0,1:T(8,128)}), f32[192,192]{0,1:T(8,128)}) %all-reduce.9.cloned.1.call-update) | async-done | bytes 147472 | tf_op jit(solution)/shard_map/psum | solution.py:26
  164.5 1.0 copy.9
  166.6 11.7 %cholesky.51 = f32[128,128]{1,0:T(8,128)S(1)} custom-call(f32[128,128]{1,0:T(8,128)S(1)} %cholesky.124), custom_call_target="Cholesky" | custom-call | tf_op jit(solution)/shard_map/jit(cholesky)/cholesky | solution.py:33
  178.9 10.4 %custom-call.18 = f32[1,128,128]{1,2,0:T(8,128)} custom-call(f32[1,128,128]{2,1,0:T(8,128)S(1)} %get-tuple-element.23), custom_call_target="InvertDiagBlocksLowerTriangular" | custom-call | tf_op jit(solution)/shard_map/jit(cholesky)/cholesky | solution.py:33
  190.2 1.0 constant_dynamic-update-slice_fusion
  192.1 6.6 %cholesky.110 = f32[64,64]{1,0:T(8,128)S(1)} custom-call(f32[64,64]{1,0:T(8,128)} %convolution_subtract_fusion.2), custom_call_target="Cholesky" | custom-call | tf_op jit(solution)/shard_map/jit(cholesky)/cholesky | solution.py:33
  202.2 20.5 %custom-call.19 = f32[2,128,128]{1,2,0:T(8,128)S(1)} custom-call(f32[2,128,128]{2,1,0:T(8,128)} %pad_maximum_fusion), custom_call_target="InvertDiagBlocksLowerTriangular" | custom-call | tf_op jit(solution)/shard_map/jit(_cho_solve)/triangular_solve | solution.py:34
  222.7 1.4 fusion.11
  224.1 1.2 convolution_subtract_fusion.1
  225.7 1.0 fusion.22
  227.1 1.2 fusion.19
  228.3 87.9 %all-reduce.7.cloned.1.call-done = bf16[2048,192]{0,1:T(8,128)(2,1)} async-done(((bf16[2048,192]{0,1:T(8,128)(2,1)}), bf16[2048,192]{0,1:T(8,128)(2,1)}) %all-reduce.7.cloned.1.call-update) | async-done | bytes 786448 | tf_op jit(solution)/shard_map/psum | solution.py:30
  316.2 5.1 %mul.27 = f32[2048,4,128]{2,1,0:T(4,128)S(1)} broadcast(f32[2048,4]{1,0:T(8,128)} %copy.12), dimensions={0,1} | broadcast | bytes 4227072 | tf_op jit(solution)/shard_map/mul | solution.py:44
  321.3 3.7 fusion.27
  325.0 2.4 convert_bitcast_fusion
  327.4 56.3 %all_to_all.5 = bf16[32,32,2048]{2,1,0:T(8,128)(2,1)S(1)} all-to-all(bf16[32,32,2048]{2,1,0:T(8,128)(2,1)S(1)} %convert_bitcast_fusion), channel_id=1, replica_groups=mesh['rows'=4,'cols'=32] {'cols'}, dimensions={0} | all-to-all | bytes 8388608 | tf_op jit(solution)/shard_map/all_to_all | solution.py:55
  383.7 1.5 convert_reduce_fusion
  (47 shorter events, 10.6 us)
Async XLA Ops:
  7.2 317.8 %copy-start = (bf16[1024,512]{1,0:T(8,128)(2,1)S(1)}, bf16[1024,512]{1,0:T(8,128)(2,1)}, u32[]{:S(2)}) copy-start(bf16[1024,512]{1,0:T(8,128)(2,1)} %param.11) | copy-start | bytes 3145732
  7.2 10.4 %copy-start.1 = (bf16[2048,512]{1,0:T(8,128)(2,1)S(1)}, bf16[2048,512]{1,0:T(8,128)(2,1)}, u32[]{:S(2)}) copy-start(bf16[2048,512]{1,0:T(8,128)(2,1)} %param.6) | copy-start | bytes 6291460
  7.2 157.3 %all-reduce.9.cloned.1.call-start = ((), (), s32[]{:S(2)}) async-start(), calls=%async_computation.2 | async-start | bytes 393216 | tf_op jit(solution)/shard_map/psum | solution.py:26
  15.5 1.4 copy-start.2
  16.8 8.9 %copy-start.6 = (s32[2048]{0:T(1024)S(1)}, s32[2048]{0:T(1024)}, u32[]{:S(2)}) copy-start(s32[2048]{0:T(1024)} %param.10) | copy-start | bytes 24580
  16.8 206.0 %all-reduce.11.cloned.1.call-start = ((), (), s32[]{:S(2)}) async-start(), calls=%async_computation.3 | async-start | bytes 786432 | tf_op jit(solution)/shard_map/psum | solution.py:29
  17.5 298.7 %all-reduce.7.cloned.1.call-start = ((), (), s32[]{:S(2)}) async-start(), calls=%async_computation.1 | async-start | bytes 1572864 | tf_op jit(solution)/shard_map/psum | solution.py:30
  178.3 0.7 copy-start.5
  222.7 2.6 copy-start.4
  316.2 5.1 %copy-start.3 = (bf16[2048,192]{0,1:T(8,128)(2,1)S(1)}, bf16[2048,192]{0,1:T(8,128)(2,1)}, u32[]{:S(2)}) copy-start(bf16[2048,192]{0,1:T(8,128)(2,1)} %all-reduce.7.cloned.1.call-done) | copy-start | bytes 2359300
Sparse Core Ops, SparseCore 0:
  16.9 147.6 all-reduce.8
  166.9 38.7 all-reduce.10
  209.0 107.2 all-reduce.6

commit v2 on v1

--- a/solution.py
+++ b/solution.py
@@ -1,9 +1,255 @@
+import functools
+
 import jax
 import jax.numpy as jnp
 from jax import lax
+from jax.experimental import pallas as pl
+from jax.experimental.pallas import tpu as pltpu
 from jax.sharding import PartitionSpec as P
 
 BLK = 128
+LANES = 256
+MESH = pl.DeviceIdType.MESH
+HIGHEST = lax.Precision.HIGHEST
+
+
+def aligned(value, factor):
+    return pl.multiple_of(value, factor)
+
+
+def place():
+    row = lax.axis_index("rows")
+    col = lax.axis_index("cols")
+    core = lax.rem(col, 2)
+    z = lax.rem(col // 2, 4)
+    y = col // 8
+    partner = (row, col + 1 - 2 * core)
+    axes = {
+        "x": (row, lambda j: (j, col)),
+        "y": (y, lambda j: (row, (j * 4 + z) * 2 + core)),
+        "z": (z, lambda j: (row, (y * 4 + j) * 2 + core)),
+    }
+    return core, partner, axes
+
+
+def enter(partner, axes):
+    barrier = pltpu.get_barrier_semaphore()
+    pl.semaphore_signal(barrier, inc=1, device_id=partner, device_id_type=MESH)
+    for index, device in axes.values():
+        for step in (1, 2, 3):
+            pl.semaphore_signal(
+                barrier, inc=1, device_id=device(lax.rem(index + step, 4)), device_id_type=MESH
+            )
+    pl.semaphore_wait(barrier, 1 + 3 * len(axes))
+
+
+def exchange_kernel(
+    own_ref, weight_ref, line_ref, square_ref, panel_ref, chosen_ref,
+    square_part, half_rx, half, z_rx, z_sum, y_rx, y_sum, x_rx,
+    panel_rx, weight_part, weight_rx, weight_half, first_rx, first_sum, second_rx,
+    send_sem, recv_sem,
+):
+    core, partner, axes = place()
+    col_offset = lax.axis_index("cols") * weight_ref.shape[1]
+    count = own_ref.shape[0]
+    half_rows = count // 2
+    quarter = half_rows // 4
+    started = []
+
+    def send(src, dst, stage, slot, device):
+        copy = pltpu.make_async_remote_copy(
+            src_ref=src, dst_ref=dst, send_sem=send_sem.at[stage, slot], recv_sem=recv_sem.at[stage, slot],
+            device_id=device, device_id_type=MESH,
+        )
+        copy.start()
+        started.append(copy)
+        return copy
+
+    def scatter(axis, src, base, piece, rx, stage):
+        index, device = axes[axis]
+        copies = []
+        for step in (1, 2, 3):
+            peer = lax.rem(index + step, 4)
+            start = aligned(base + peer * piece, 8)
+            copies.append(send(src.at[pl.ds(start, piece)], rx.at[step - 1], stage, step - 1, device(peer)))
+        return copies
+
+    def spread(axis, src, dst_of, stage):
+        index, device = axes[axis]
+        return [
+            send(src, dst_of(step - 1), stage, step - 1, device(lax.rem(index + step, 4))) for step in (1, 2, 3)
+        ]
+
+    def arrive(copies):
+        for copy in copies:
+            copy.wait_recv()
+
+    def total(own, rx):
+        return own + rx[0] + rx[1] + rx[2]
+
+    enter(partner, axes)
+
+    x, y, z = axes["x"][0], axes["y"][0], axes["z"][0]
+    lines = lax.broadcasted_iota(jnp.int32, (weight_ref.shape[1], LANES), 0) + col_offset
+    onehot = jnp.where(lines == line_ref[0:1, :], 1.0, 0.0)
+    square_part[...] = jnp.dot(own_ref[...], onehot, precision=HIGHEST, preferred_element_type=jnp.float32)
+    s1 = send(
+        square_part.at[pl.ds(aligned((1 - core) * half_rows, 8), half_rows)], half_rx, 0, 0, partner
+    )
+    panel_piece = count // 4
+    p1 = scatter("x", own_ref, 0, panel_piece, panel_rx, 1)
+    weight_part[...] = jnp.dot(
+        weight_ref[...], onehot.astype(jnp.bfloat16), preferred_element_type=jnp.float32
+    ).astype(jnp.bfloat16)
+    rows = weight_ref.shape[0]
+    share = rows // 2
+    w1 = send(weight_part.at[pl.ds(aligned((1 - core) * share, 16), share)], weight_rx, 2, 0, partner)
+    s1.wait_recv()
+    half[...] = square_part[pl.ds(aligned(core * half_rows, 8), half_rows), :] + half_rx[...]
+    s2 = scatter("z", half, 0, quarter, z_rx, 3)
+    arrive(s2)
+    z_sum[...] = total(half[pl.ds(aligned(z * quarter, 8), quarter), :], z_rx)
+    s3 = spread("y", z_sum, lambda slot: y_rx.at[slot], 4)
+    w1.wait_recv()
+    weight_half[...] = weight_part[pl.ds(aligned(core * share, 16), share), :] + weight_rx[...]
+    arrive(s3)
+    y_sum[...] = total(z_sum[...], y_rx)
+    s4 = spread("x", y_sum, lambda slot: x_rx.at[slot], 5)
+    part = share // 2
+    piece = part // 4
+    small = piece // 4
+    wa = scatter("y", weight_half, 0, piece, first_rx.at[0], 6)
+    wb = scatter("z", weight_half, part, piece, first_rx.at[1], 7)
+    arrive(s4)
+    mine = pl.ds(aligned(core * half_rows + z * quarter, 8), quarter)
+    square_ref[mine, :] = total(y_sum[...], x_rx)
+    s5 = spread("z", square_ref.at[mine], lambda slot: square_ref.at[mine], 8)
+    arrive(p1)
+    own_panel = pl.ds(aligned(x * panel_piece, 8), panel_piece)
+    panel_ref[own_panel, :] = total(own_ref[own_panel, :], panel_rx)
+    p2 = spread("x", panel_ref.at[own_panel], lambda slot: panel_ref.at[own_panel], 9)
+    arrive(s5)
+    own_half = pl.ds(aligned(core * half_rows, 8), half_rows)
+    s6 = send(square_ref.at[own_half], square_ref.at[own_half], 10, 0, partner)
+    arrive(wa)
+    first_sum[0] = total(weight_half[pl.ds(aligned(y * piece, 16), piece), :], first_rx.at[0])
+    wa = scatter("z", first_sum.at[0], 0, small, second_rx.at[0], 11)
+    arrive(wb)
+    first_sum[1] = total(weight_half[pl.ds(aligned(part + z * piece, 16), piece), :], first_rx.at[1])
+    wb = scatter("y", first_sum.at[1], 0, small, second_rx.at[1], 12)
+    arrive(wa)
+    base_a = core * share + y * piece
+    base_b = core * share + part + z * piece
+    slice_a = pl.ds(aligned(base_a + z * small, 16), small)
+    slice_b = pl.ds(aligned(base_b + y * small, 16), small)
+    chosen_ref[slice_a, :] = total(first_sum[0, pl.ds(aligned(z * small, 16), small), :], second_rx.at[0])
+    wa = spread("z", chosen_ref.at[slice_a], lambda slot: chosen_ref.at[slice_a], 13)
+    arrive(wb)
+    chosen_ref[slice_b, :] = total(first_sum[1, pl.ds(aligned(y * small, 16), small), :], second_rx.at[1])
+    wb = spread("y", chosen_ref.at[slice_b], lambda slot: chosen_ref.at[slice_b], 14)
+    arrive(wa)
+    piece_a = pl.ds(aligned(base_a, 16), piece)
+    wa = spread("y", chosen_ref.at[piece_a], lambda slot: chosen_ref.at[piece_a], 15)
+    arrive(wb)
+    piece_b = pl.ds(aligned(base_b, 16), piece)
+    wb = spread("z", chosen_ref.at[piece_b], lambda slot: chosen_ref.at[piece_b], 16)
+    arrive(wa)
+    arrive(wb)
+    own_share = pl.ds(aligned(core * share, 16), share)
+    w6 = send(chosen_ref.at[own_share], chosen_ref.at[own_share], 17, 0, partner)
+    arrive(p2)
+    s6.wait_recv()
+    w6.wait_recv()
+    for copy in started:
+        copy.wait_send()
+
+
+def exchange(own_rows, weight, line):
+    count, columns = own_rows.shape
+    rows = weight.shape[0]
+    f32, bf16 = jnp.float32, jnp.bfloat16
+    half, quarter = count // 2, count // 8
+    share = rows // 2
+    piece = share // 8
+    small = piece // 4
+    vmem = pl.BlockSpec(memory_space=pltpu.VMEM)
+    return pl.pallas_call(
+        exchange_kernel,
+        out_shape=(
+            jax.ShapeDtypeStruct((count, LANES), f32),
+            jax.ShapeDtypeStruct((count, columns), f32),
+            jax.ShapeDtypeStruct((rows, LANES), bf16),
+        ),
+        in_specs=[vmem] * 3,
+        out_specs=(vmem,) * 3,
+        scratch_shapes=[
+            pltpu.VMEM((count, LANES), f32),
+            pltpu.VMEM((half, LANES), f32),
+            pltpu.VMEM((half, LANES), f32),
+            pltpu.VMEM((3, quarter, LANES), f32),
+            pltpu.VMEM((quarter, LANES), f32),
+            pltpu.VMEM((3, quarter, LANES), f32),
+            pltpu.VMEM((quarter, LANES), f32),
+            pltpu.VMEM((3, quarter, LANES), f32),
+            pltpu.VMEM((3, count // 4, columns), f32),
+            pltpu.VMEM((rows, LANES), bf16),
+            pltpu.VMEM((share, LANES), bf16),
+            pltpu.VMEM((share, LANES), bf16),
+            pltpu.VMEM((2, 3, piece, LANES), bf16),
+            pltpu.VMEM((2, piece, LANES), bf16),
+            pltpu.VMEM((2, 3, small, LANES), bf16),
+            pltpu.SemaphoreType.DMA((18, 3)),
+            pltpu.SemaphoreType.DMA((18, 3)),
+        ],
+        compiler_params=pltpu.CompilerParams(
+            collective_id=0, has_side_effects=True, vmem_limit_bytes=40 << 20
+        ),
+        name="exchange",
+    )(own_rows, weight, line)
+
+
+def invert_kernel(square_ref, panel_ref, coeffs_ref, state):
+    count = square_ref.shape[0]
+    side = 64
+    state[...] = square_ref[...]
+    lane = lax.broadcasted_iota(jnp.int32, (side, BLK), 1)
+    line = lax.broadcasted_iota(jnp.int32, (side, BLK), 0)
+    for block in range(count // side):
+        lo = block * side
+        tile = state[lo : lo + side, (lo // BLK) * BLK : (lo // BLK) * BLK + BLK]
+        shift = lo % BLK
+        for k in range(side):
+            pivot_row = tile[k : k + 1, :]
+            column = jnp.take_along_axis(tile, jnp.full((side, BLK), k + shift, jnp.int32), axis=1)
+            scale = 1.0 / column[k : k + 1, :]
+            scaled = jnp.where(lane[0:1, :] == k + shift, scale, pivot_row * scale)
+            kept = jnp.where(lane == k + shift, 0.0, tile)
+            tile = jnp.where(line == k, scaled, kept - column * scaled)
+        inverse = tile[:, shift : shift + side]
+        strip = state[:, lo : lo + side]
+        lanes = lax.broadcasted_iota(jnp.int32, (side, LANES), 1)
+        inside = (lanes >= lo) & (lanes < lo + side)
+        unit = jnp.where(lanes - lo == lax.broadcasted_iota(jnp.int32, (side, LANES), 0), 1.0, 0.0)
+        right = jnp.where(inside, unit, state[lo : lo + side, :])
+        right = jnp.dot(inverse, right, precision=HIGHEST, preferred_element_type=jnp.float32)
+        all_lanes = lax.broadcasted_iota(jnp.int32, (count, LANES), 1)
+        cleared = jnp.where((all_lanes >= lo) & (all_lanes < lo + side), 0.0, state[...])
+        state[...] = cleared - jnp.dot(strip, right, precision=HIGHEST, preferred_element_type=jnp.float32)
+        state[lo : lo + side, :] = right
+    coeffs_ref[...] = jnp.dot(
+        state[:, :count], panel_ref[...], precision=HIGHEST, preferred_element_type=jnp.float32
+    )
+
+
+def solve(square, panel):
+    return pl.pallas_call(
+        invert_kernel,
+        out_shape=jax.ShapeDtypeStruct(panel.shape, jnp.float32),
+        in_specs=[pl.BlockSpec(memory_space=pltpu.VMEM)] * 2,
+        out_specs=pl.BlockSpec(memory_space=pltpu.VMEM),
+        scratch_shapes=[pltpu.VMEM(square.shape, jnp.float32)],
+        name="solve",
+    )(square, panel)
 
 
 def local(weight, hess_inv, selected, block_mask, row_limits, calibration):
@@ -11,8 +257,8 @@
     out_local = weight.shape[0]
     group = lax.axis_size("cols")
     row_offset = lax.axis_index("rows") * rows_local
-    col_offset = lax.axis_index("cols") * cols_local
     chosen = selected.reshape(-1)
+    count = chosen.shape[0]
     row_place = chosen - row_offset
     row_inside = (row_place >= 0) & (row_place < rows_local)
     own_rows = jnp.where(
@@ -20,20 +266,11 @@
         jnp.take(hess_inv, jnp.clip(row_place, 0, rows_local - 1), axis=0),
         0.0,
     )
-    onehot = (
-        lax.broadcasted_iota(jnp.int32, (cols_local, chosen.shape[0]), 0) == (chosen - col_offset)[None, :]
-    )
-    square = lax.psum(
-        jnp.dot(own_rows, onehot.astype(jnp.float32), precision=lax.Precision.HIGHEST), ("rows", "cols")
-    )
-    panel = lax.psum(own_rows, "rows")
-    weight_cols = lax.psum(
-        jnp.dot(weight, onehot.astype(jnp.bfloat16), preferred_element_type=jnp.float32).astype(jnp.bfloat16), "cols"
-    )
-    factor = jnp.linalg.cholesky(square)
-    coeffs = jax.scipy.linalg.cho_solve((factor, True), panel)
+    line = jnp.broadcast_to(jnp.pad(chosen, (0, LANES - count), constant_values=-1)[None, :], (8, LANES))
+    square, panel, weight_cols = exchange(own_rows, weight, line)
+    coeffs = solve(square, panel)
     wide = weight.astype(jnp.float32)
-    refit = wide - jnp.dot(weight_cols.astype(jnp.float32), coeffs, precision=lax.Precision.HIGHEST)
+    refit = wide - jnp.dot(weight_cols[:, :count].astype(jnp.float32), coeffs, precision=HIGHEST)
     blocks_local = cols_local // BLK
     running_count = jnp.cumsum(block_mask, axis=1)
     retained = block_mask * (running_count <= row_limits[:, None]).astype(jnp.int32)

time: 393 us -> 146 us (0.37)
  waiting for transfers between devices: 225 us -> 0 us
  Pallas kernels: 0 us -> 60.9 us
  other arithmetic: 61.9 us -> 6.41 us
  between operations: 15.2 us -> 0.75 us
  matrix products: 16.5 us -> 5.97 us
    psum x3 -> x0, waiting for transfers between devices: 225 us -> none  [the longest x1 137 us: local(): lax.psum(jnp.dot(own_rows, onehot.astype(jnp.float32), precision=lax.Prec...]
    pallas_call x0 -> x2, Pallas kernels: none -> 60.9 us  [the longest x1 40.4 us: exchange(): pl.pallas_call(exchange_kernel, out_shape=(jax.ShapeDtypeStruct((count, L...]
    another operation x13 -> x0, other arithmetic: 52.8 us -> none  [the longest x7 30.1 us: local(): factor = jnp.linalg.cholesky(square)]
    another operation x8 -> x0, matrix products: 7.35 us -> none  [the longest x6 5.53 us: local(): coeffs = jax.scipy.linalg.cho_solve((factor, True), panel)]
  transfers between devices with their start and end apart: 3 -> 0, of which waited for: 2 -> 0; matrix products, arithmetic and copies ran while one was open for 19% -> 0% of each run, Pallas kernels for 0% -> 0%
where the time goes in v2:
time: 146 us
  Pallas kernels  60.9 us (42%)
  blocking collectives  54.9 us (38%)
  local copies, waits for them, and re-layouts  16.7 us (11%)
  other arithmetic  6.41 us (4%)
  matrix products  5.97 us (4%)
    all_to_all x1, blocking collectives, local(): lax.all_to_all(partial, 'cols', split_axis=0, concat_axis=0, tiled=True)  54.9 us
    pallas_call x1, Pallas kernels, exchange(): pl.pallas_call(exchange_kernel, out_shape=(jax.ShapeDtypeStruct((count, L...  40.4 us
    pallas_call x1, Pallas kernels, solve(): pl.pallas_call(invert_kernel, out_shape=jax.ShapeDtypeStruct(panel.shape,...  20.6 us
    mul x1, local copies, waits for them, and re-layouts, local(): refit.reshape(out_local, blocks_local, BLK)  5.1 us
    unnamed x17, local copies, waits for them, and re-layouts  4.93 us
    gather x1, local copies, waits for them, and re-layouts, local(): jnp.take(hess_inv, jnp.clip(row_place, 0, rows_local - 1), axis=0)  4.42 us
    dot_general x1, matrix products, local(): jnp.dot(weight_cols[:, :count].astype(jnp.float32), coeffs, precision=HIG...  3.56 us
    another operation x1, other arithmetic, local(): running_count = jnp.cumsum(block_mask, axis=1)  3.22 us

profile of v2, /device:TPU:1, one launch (start us, length us, event | category | flops | bytes accessed | tf_op | source)
XLA Modules:
  0.0 145.7 jit_solution(3142952413306165606)
XLA Ops:
  0.6 0.0 copy-start
  0.6 0.0 copy-start.7
  0.7 0.8 reshape.55
  1.5 0.7 subtract_clamp_fusion
  2.2 0.1 min.18
  2.3 2.5 %copy.8 = s32[2048,128]{0,1:T(8,128)} copy(s32[2048,128]{1,0:T(8,128)} %param.9) | data formatting | bytes 2097152 | tf_op args[3]
  4.9 3.2 %reduce_window_sum.11 = s32[2048,128]{0,1:T(8,128)} reduce-window(s32[2048,128]{0,1:T(8,128)} %copy.8, s32[]{:T(128)} %constant.15.clone.1), window={size=1x128 pad=0_0x127_0}, to_apply=%region_0.1 | reduce-window | flops 33292288 | bytes 2097156 | tf_op jit(solution)/shard_map/jit(cumsum)/reduce_window_sum | solution.py:275
  8.1 0.0 copy-done.7
  8.1 0.9 fusion.5
  9.0 1.3 copy.10
  10.3 4.4 %gather_fusion = f32[192,512]{1,0:T(8,128)S(1)} fusion(f32[4096,512]{1,0:T(8,128)} %param.7, s32[1024]{0:T(1024)S(1)} %pad_clamp_fusion), kind=kCustom, calls=%fused_computation | custom fusion | bytes 787200 | tf_op jit(solution)/shard_map/jit(_take)/gather | solution.py:266
  14.7 0.1 select_select_fusion.own_ref
  14.9 0.0 copy-done.1
  14.9 40.4 %exchange.1 = (f32[192,256]{1,0:T(8,128)S(1)}, f32[192,512]{1,0:T(8,128)S(1)}, bf16[2048,256]{1,0:T(8,128)(2,1)S(1)}) custom-call(f32[192,512]{1,0:T(8,128)S(1)} %select_select_fusion.own_ref, bf16[2048,512]{1,0:T(8,128)(2,1)S(1)} %copy-done.1, s32[8,256]{1,0:T(8,128)S(1)} %broadcast_in_dim.35.line_ref), custom_call_target="tpu_custom_call" | custom-call | tf_op jit(solution)/shard_map/exchange/pallas_call | solution.py:176
  55.3 1.0 copy-done.2
  56.3 0.7 copy-done.4
  57.0 0.7 copy-done.5
  57.7 20.6 %solve.1 = f32[192,512]{1,0:T(8,128)} custom-call(f32[192,256]{1,0:T(8,128)} %copy-done.5, f32[192,512]{1,0:T(8,128)} %copy-done.4), custom_call_target="tpu_custom_call" | custom-call | tf_op jit(solution)/shard_map/solve/pallas_call | solution.py:245
  78.2 5.1 %mul.23 = f32[2048,4,128]{2,1,0:T(4,128)S(1)} broadcast(f32[2048,4]{1,0:T(8,128)} %copy.10), dimensions={0,1} | broadcast | bytes 4227072 | tf_op jit(solution)/shard_map/mul | solution.py:281
  83.4 3.6 %fusion.6 = (bf16[2048,512]{1,0:T(8,128)(2,1)}, f32[2048,512]{1,0:T(8,128)S(1)}) fusion(f32[256,8,4,128]{3,2,1,0:T(4,128)S(1)} %bitcast.14, f32[192,512]{1,0:T(8,128)S(1)} %copy-done.6, bf16[2048,256]{1,0:T(8,128)(2,1)S(1)} %copy-done.3, bf16[2048,512]{1,0:T(8,128)(2,1)S(1)} %copy-done.1), kind=kOutput, calls=%fused_computation.19 | convolution fusion | flops 2420113408 | bytes 14024704 | tf_op jit(solution)/shard_map/dot_general | solution.py:273
  86.9 0.0 copy-done
  86.9 2.4 %convert_bitcast_fusion = bf16[32,32,2048]{2,1,0:T(8,128)(2,1)S(1)} fusion(bf16[32,32,512]{2,1,0:T(8,128)(2,1)S(1)} %bitcast.13, f32[2048,512]{1,0:T(8,128)S(1)} %get-tuple-element.11, bf16[2048,512]{1,0:T(8,128)(2,1)S(1)} %copy-done.1), kind=kOutput, calls=%fused_computation.6 | convolution fusion | flops 2152726528 | bytes 11534336 | tf_op jit(solution)/shard_map/dot_general | solution.py:286
  89.3 54.9 %all_to_all.5 = bf16[32,32,2048]{2,1,0:T(8,128)(2,1)S(1)} all-to-all(bf16[32,32,2048]{2,1,0:T(8,128)(2,1)S(1)} %convert_bitcast_fusion), channel_id=1, replica_groups=mesh['rows'=4,'cols'=32] {'cols'}, dimensions={0} | all-to-all | bytes 8388608 | tf_op jit(solution)/shard_map/all_to_all | solution.py:292
  144.3 1.5 %convert_reduce_fusion = f32[32,2048]{1,0:T(8,128)} fusion(bf16[32,32,2048]{2,1,0:T(8,128)(2,1)S(1)} %all_to_all.5), kind=kLoop, calls=%fused_computation.1 | loop fusion | flops 4128768 | bytes 4456448 | tf_op jit(solution)/shard_map/reduce_sum | solution.py:293
  (13 shorter events, 0.0 us)
Async XLA Ops:
  0.6 86.3 %copy-start = (bf16[1024,512]{1,0:T(8,128)(2,1)S(1)}, bf16[1024,512]{1,0:T(8,128)(2,1)}, u32[]{:S(2)}) copy-start(bf16[1024,512]{1,0:T(8,128)(2,1)} %param.11) | copy-start | bytes 3145732
  0.6 7.4 %copy-start.7 = (s32[2048]{0:T(1024)S(1)}, s32[2048]{0:T(1024)}, u32[]{:S(2)}) copy-start(s32[2048]{0:T(1024)} %param.10) | copy-start | bytes 24580
  4.9 10.0 %copy-start.1 = (bf16[2048,512]{1,0:T(8,128)(2,1)S(1)}, bf16[2048,512]{1,0:T(8,128)(2,1)}, u32[]{:S(2)}) copy-start(bf16[2048,512]{1,0:T(8,128)(2,1)} %weight_ref.1) | copy-start | bytes 6291460
  55.3 1.0 copy-start.2
  56.3 0.7 copy-start.4
  57.0 0.7 copy-start.5
  78.2 5.1 %copy-start.3 = (bf16[2048,256]{1,0:T(8,128)(2,1)S(1)}, bf16[2048,256]{1,0:T(8,128)(2,1)}, u32[]{:S(2)}) copy-start(bf16[2048,256]{1,0:T(8,128)(2,1)} %copy-done.2) | copy-start | bytes 3145732
  78.2 5.1 %copy-start.6 = (f32[192,512]{1,0:T(8,128)S(1)}, f32[192,512]{1,0:T(8,128)}, u32[]{:S(2)}) copy-start(f32[192,512]{1,0:T(8,128)} %solve.1) | copy-start | bytes 1179652

commit v3 on v2

--- a/solution.py
+++ b/solution.py
@@ -252,10 +252,221 @@
     )(square, panel)
 
 
+def reduce_kernel(
+    weight_ref, chosen_ref, coeffs_ref, mask_ref, limit_ref, features_ref, pruned_ref, error_ref,
+    high, low, features_rx, own_diff, sent_diff, diff_rx, part, forward_rx, forward, ring_rx,
+    sums, sums_wide, small_forward_rx, small_forward, small_rx, final,
+    send_sem, recv_sem,
+):
+    core, partner, axes = place()
+    axes = {name: axes[name] for name in ("y", "z")}
+    rows, columns = weight_ref.shape
+    share = rows // 2
+    chunks = part.shape[0]
+    chunk = share // chunks
+    blocks = columns // BLK
+    tokens_axis = part.shape[1]
+    first_block = lax.axis_index("cols") * blocks
+    started = []
+
+    def remote(src, dst, stage, slot, device):
+        return pltpu.make_async_remote_copy(
+            src_ref=src, dst_ref=dst, send_sem=send_sem.at[stage, slot], recv_sem=recv_sem.at[stage, slot],
+            device_id=device, device_id_type=MESH,
+        )
+
+    def send(*args):
+        copy = remote(*args)
+        copy.start()
+        started.append(copy)
+        return copy
+
+    enter(partner, axes)
+    features_copy = send(features_ref, features_rx, 0, 0, partner)
+
+    coeffs = coeffs_ref[...]
+    high[...] = coeffs.astype(jnp.bfloat16)
+    low[...] = (coeffs - high[...].astype(jnp.float32)).astype(jnp.bfloat16)
+    count = coeffs_ref.shape[0]
+    line = lax.broadcasted_iota(jnp.int32, (BLK, columns), 0)
+    block = first_block + lax.broadcasted_iota(jnp.int32, (BLK, columns), 1) // BLK
+    before = jnp.where(line <= block, 1.0, 0.0).astype(jnp.bfloat16)
+    here = jnp.where(line == block, 1.0, 0.0).astype(jnp.bfloat16)
+    spread = jnp.where(lax.broadcasted_iota(jnp.int32, (16, columns), 0) == 0, 1.0, 0.0).astype(jnp.bfloat16)
+
+    def differ(first, store):
+        lines = pl.ds(aligned(first, chunk), chunk)
+        picked = chosen_ref[lines, :][:, :count]
+        change = jnp.dot(picked, high[...], preferred_element_type=jnp.float32)
+        change += jnp.dot(picked, low[...], preferred_element_type=jnp.float32)
+        mask = mask_ref[lines, :].astype(jnp.float32).astype(jnp.bfloat16)
+        seen = jnp.dot(mask, before, preferred_element_type=jnp.float32)
+        bit = jnp.dot(mask, here, preferred_element_type=jnp.float32)
+        limit = lax.dot_general(
+            limit_ref[:, lines], spread, (((0,), (0,)), ((), ())), preferred_element_type=jnp.float32
+        )
+        kept = jnp.where(seen <= limit, bit, 0.0)
+        wide = weight_ref[lines, :].astype(jnp.float32)
+        masked = (wide - change) * kept
+        pruned_ref[lines, :] = masked.astype(jnp.bfloat16)
+        store((wide - masked).astype(jnp.bfloat16))
+
+    def diff_copy(i):
+        lines = pl.ds(aligned(i * chunk, chunk), chunk)
+        return remote(sent_diff.at[lines], diff_rx.at[lines], 1, i, partner)
+
+    @pl.loop(0, chunks)
+    def _(i):
+        def store(value):
+            sent_diff[pl.ds(aligned(i * chunk, chunk), chunk), :] = value
+
+        differ((1 - core) * share + i * chunk, store)
+        diff_copy(i).start()
+
+    @pl.loop(0, chunks)
+    def _(i):
+        def store(value):
+            own_diff[pl.ds(aligned(i * chunk, chunk), chunk), :] = value
+
+        differ(core * share + i * chunk, store)
+
+    features_copy.wait_recv()
+
+    def multiply(k):
+        lines = pl.ds(k * chunk, chunk)
+        tokens = features_ref.shape[0] // tokens_axis
+
+        @pl.loop(0, tokens_axis)
+        def _(t):
+            words = pl.ds(aligned(t * tokens, tokens), tokens)
+            product = lax.dot_general(
+                features_ref[words, :], own_diff[lines, :], (((1,), (1,)), ((), ())),
+                preferred_element_type=jnp.float32,
+            )
+            product += lax.dot_general(
+                features_rx[words, :], diff_rx[lines, :], (((1,), (1,)), ((), ())),
+                preferred_element_type=jnp.float32,
+            )
+            part[k, t] = product.astype(jnp.bfloat16).reshape(part.shape[2:])
+
+    def ring(axis, sent, value, extent, through_rx, through, rx, stage):
+        index, device = axes[axis]
+        right, left, across = lax.rem(index + 1, 4), lax.rem(index + 3, 4), lax.rem(index + 2, 4)
+        lo, hi = pl.ds(0, extent // 2), pl.ds(extent // 2, extent // 2)
+        a = send(sent(across).at[lo], through_rx.at[0], stage, 0, device(right))
+        b = send(sent(across).at[hi], through_rx.at[1], stage, 1, device(left))
+        c = send(sent(right).at[hi], rx.at[0, hi], stage, 2, device(right))
+        d = send(sent(left).at[lo], rx.at[1, lo], stage, 3, device(left))
+        later = []
+
+        def pass_on():
+            a.wait_recv()
+            through[0] = (value(right, lo) + through_rx[0].astype(jnp.float32)).astype(jnp.bfloat16)
+            later.append(send(through.at[0], rx.at[0, lo], stage, 4, device(right)))
+            b.wait_recv()
+            through[1] = (value(left, hi) + through_rx[1].astype(jnp.float32)).astype(jnp.bfloat16)
+            later.append(send(through.at[1], rx.at[1, hi], stage, 5, device(left)))
+
+        def finish():
+            for copy in (c, d, *later):
+                copy.wait_recv()
+            return value(index, pl.ds(0, extent)) + rx[0].astype(jnp.float32) + rx[1].astype(jnp.float32)
+
+        return pass_on, finish
+
+    order = [k for pair in zip(range(chunks // 2), range(chunks // 2, chunks)) for k in pair]
+    rings = {}
+    for k in order:
+        diff_copy(k).wait_recv()
+        multiply(k)
+        if k < chunks // 2:
+            axis = "y"
+            sent = functools.partial(lambda k, j: part.at[k, j], k)
+        else:
+            axis = "z"
+            sent = functools.partial(lambda k, j: part.at[k, :, j], k)
+        value = functools.partial(lambda sent, j, which: sent(j).at[which][...].astype(jnp.float32), sent)
+        rings[k] = ring(axis, sent, value, 4, forward_rx.at[k], forward.at[k], ring_rx.at[k], 2 + k)
+    for k in order:
+        rings[k][0]()
+    again = {}
+    for k in order:
+        total = rings[k][1]()
+        sums_wide[k] = total
+        sums[k] = total.astype(jnp.bfloat16)
+        axis = "z" if k < chunks // 2 else "y"
+        sent = functools.partial(lambda k, j: sums.at[k, j], k)
+        value = functools.partial(lambda k, j, which: sums_wide[k, j, which, :], k)
+        again[k] = ring(
+            axis, sent, value, 64, small_forward_rx.at[k], small_forward.at[k], small_rx.at[k], 2 + chunks + k
+        )
+    for k in order:
+        again[k][0]()
+    tokens = error_ref.shape[0]
+    last = []
+    for k in order:
+        final[k] = again[k][1]()
+        lanes = pl.ds(aligned(core * share + k * chunk, chunk), chunk)
+        last.append(
+            send(
+                final.at[k, pl.ds(aligned((1 - core) * tokens, tokens), tokens)],
+                error_ref.at[:, lanes], 2 + 2 * chunks, k, partner,
+            )
+        )
+        error_ref[:, lanes] = final[k, pl.ds(aligned(core * tokens, tokens), tokens), :]
+    for copy in last:
+        copy.wait_recv()
+    for i in range(chunks):
+        diff_copy(i).wait_send()
+    for copy in started:
+        copy.wait_send()
+
+
+def reduce_error(weight, chosen, coeffs, mask, limit, features):
+    rows, columns = weight.shape
+    tokens = features.shape[0]
+    f32, bf16 = jnp.float32, jnp.bfloat16
+    share, chunks = rows // 2, 4
+    chunk = share // chunks
+    vmem = pl.BlockSpec(memory_space=pltpu.VMEM)
+    return pl.pallas_call(
+        reduce_kernel,
+        out_shape=(
+            jax.ShapeDtypeStruct((rows, columns), bf16),
+            jax.ShapeDtypeStruct((tokens // 32, rows), f32),
+        ),
+        in_specs=[vmem] * 6,
+        out_specs=(vmem,) * 2,
+        scratch_shapes=[
+            pltpu.VMEM(coeffs.shape, bf16),
+            pltpu.VMEM(coeffs.shape, bf16),
+            pltpu.VMEM(features.shape, bf16),
+            pltpu.VMEM((share, columns), bf16),
+            pltpu.VMEM((share, columns), bf16),
+            pltpu.VMEM((share, columns), bf16),
+            pltpu.VMEM((chunks, 4, 4, 64, chunk), bf16),
+            pltpu.VMEM((chunks, 2, 2, 64, chunk), bf16),
+            pltpu.VMEM((chunks, 2, 2, 64, chunk), bf16),
+            pltpu.VMEM((chunks, 2, 4, 64, chunk), bf16),
+            pltpu.VMEM((chunks, 4, 64, chunk), bf16),
+            pltpu.VMEM((chunks, 4, 64, chunk), f32),
+            pltpu.VMEM((chunks, 2, 32, chunk), bf16),
+            pltpu.VMEM((chunks, 2, 32, chunk), bf16),
+            pltpu.VMEM((chunks, 2, 64, chunk), bf16),
+            pltpu.VMEM((chunks, 64, chunk), f32),
+            pltpu.SemaphoreType.DMA((3 + 2 * chunks, 6)),
+            pltpu.SemaphoreType.DMA((3 + 2 * chunks, 6)),
+        ],
+        compiler_params=pltpu.CompilerParams(
+            collective_id=1, has_side_effects=True, vmem_limit_bytes=48 << 20
+        ),
+        name="reduce_error",
+    )(weight, chosen, coeffs, mask, limit, features)
+
+
 def local(weight, hess_inv, selected, block_mask, row_limits, calibration):
     rows_local, cols_local = hess_inv.shape
     out_local = weight.shape[0]
-    group = lax.axis_size("cols")
     row_offset = lax.axis_index("rows") * rows_local
     chosen = selected.reshape(-1)
     count = chosen.shape[0]
@@ -269,29 +480,9 @@
     line = jnp.broadcast_to(jnp.pad(chosen, (0, LANES - count), constant_values=-1)[None, :], (8, LANES))
     square, panel, weight_cols = exchange(own_rows, weight, line)
     coeffs = solve(square, panel)
-    wide = weight.astype(jnp.float32)
-    refit = wide - jnp.dot(weight_cols[:, :count].astype(jnp.float32), coeffs, precision=HIGHEST)
-    blocks_local = cols_local // BLK
-    running_count = jnp.cumsum(block_mask, axis=1)
-    retained = block_mask * (running_count <= row_limits[:, None]).astype(jnp.int32)
-    own_blocks = lax.dynamic_slice_in_dim(
-        retained, lax.axis_index("cols") * blocks_local, blocks_local, 1
-    )
-    masked = (
-        refit.reshape(out_local, blocks_local, BLK) * own_blocks.astype(jnp.float32)[:, :, None]
-    ).reshape(out_local, cols_local)
-    pruned = masked.astype(jnp.bfloat16)
-    difference = (wide - masked).astype(jnp.bfloat16)
-    tokens = calibration.shape[0]
-    partial = lax.dot_general(
-        calibration.reshape(group, tokens // group, cols_local),
-        difference,
-        (((2,), (1,)), ((), ())),
-        preferred_element_type=jnp.float32,
-    ).astype(jnp.bfloat16)
-    pieces = lax.all_to_all(partial, "cols", split_axis=0, concat_axis=0, tiled=True)
-    layer_error = jnp.sum(pieces.astype(jnp.float32), axis=0).T
-    return (pruned, layer_error)
+    limit = jnp.broadcast_to(row_limits[None, :], (16, out_local)).astype(jnp.bfloat16)
+    pruned, error = reduce_error(weight, weight_cols, coeffs, block_mask, limit, calibration)
+    return (pruned, error.T)
 
 
 def solution(mesh):

time: 146 us -> 108 us (0.74)
  blocking collectives: 54.9 us -> 0 us
  Pallas kernels: 60.9 us -> 90.6 us
  matrix products: 5.97 us -> 0 us
  other arithmetic: 6.41 us -> 2.61 us
  local copies, waits for them, and re-layouts: 16.7 us -> 14 us
    all_to_all x1 -> x0, blocking collectives: 54.9 us -> none  [local(): lax.all_to_all(partial, 'cols', split_axis=0, concat_axis=0, tiled=True)]
    pallas_call x0 -> x1, Pallas kernels: none -> 29.7 us  [reduce_error(): pl.pallas_call(reduce_kernel, out_shape=(jax.ShapeDtypeStruct((rows, colu...]
    dot_general x2 -> x0, matrix products: 5.97 us -> none  [the longest x1 3.56 us: local(): jnp.dot(weight_cols[:, :count].astype(jnp.float32), coeffs, precision=HIG...]
    mul x1 -> x0, local copies, waits for them, and re-layouts: 5.1 us -> none  [local(): refit.reshape(out_local, blocks_local, BLK)]
    another operation x1 -> x0, other arithmetic: 3.22 us -> none  [local(): running_count = jnp.cumsum(block_mask, axis=1)]
    unnamed x17 -> x18, local copies, waits for them, and re-layouts: 4.93 us -> 7.87 us
    reduce_sum x1 -> x0, other arithmetic: 1.47 us -> none  [local(): layer_error = jnp.sum(pieces.astype(jnp.float32), axis=0).T]
where the time goes in v3:
time: 108 us
  Pallas kernels  90.6 us (84%)
  local copies, waits for them, and re-layouts  14 us (13%)
  other arithmetic  2.61 us (2%)
    pallas_call x1, Pallas kernels, exchange(): pl.pallas_call(exchange_kernel, out_shape=(jax.ShapeDtypeStruct((count, L...  40.4 us
    pallas_call x1, Pallas kernels, reduce_error(): pl.pallas_call(reduce_kernel, out_shape=(jax.ShapeDtypeStruct((rows, colu...  29.7 us
    pallas_call x1, Pallas kernels, solve(): pl.pallas_call(invert_kernel, out_shape=jax.ShapeDtypeStruct(panel.shape,...  20.5 us
    unnamed x18, local copies, waits for them, and re-layouts  7.87 us
    gather x1, local copies, waits for them, and re-layouts, local(): jnp.take(hess_inv, jnp.clip(row_place, 0, rows_local - 1), axis=0)  5.31 us

profile of v3, /device:TPU:1, one launch (start us, length us, event | category | flops | bytes accessed | tf_op | source)
XLA Modules:
  0.0 108.0 jit_solution(3060323321928653072)
XLA Ops:
  0.6 0.8 reshape.48
  1.4 0.7 subtract_clamp_fusion
  2.1 0.1 min.18
  2.2 0.7 convert_element_type.3
  2.9 0.0 copy-start
  2.9 5.3 %gather_fusion = f32[192,512]{1,0:T(8,128)} fusion(f32[4096,512]{1,0:T(8,128)} %param.7, s32[1024]{0:T(1024)S(1)} %pad_clamp_fusion), kind=kCustom, calls=%fused_computation | custom fusion | bytes 787200 | tf_op jit(solution)/shard_map/jit(_take)/gather | solution.py:477
  8.2 0.0 copy-start.2
  8.2 1.2 %select_select_fusion.own_ref = f32[192,512]{1,0:T(8,128)S(1)} fusion(f32[192,512]{1,0:T(8,128)} %gather_fusion, pred[192]{0:T(512)(128)(4,1)S(1)} %get-tuple-element.13, pred[192]{0:T(512)(128)(4,1)S(1)} %get-tuple-element.12), kind=kLoop, calls=%fused_computation.1 | loop fusion | flops 196608 | bytes 786816 | tf_op jit(solution)/shard_map/jit(_where)/select_n | solution.py:475
  9.5 0.0 copy-done
  9.5 40.4 %exchange.1 = (f32[192,256]{1,0:T(8,128)S(1)}, f32[192,512]{1,0:T(8,128)S(1)}, bf16[2048,256]{1,0:T(8,128)(2,1)S(1)}) custom-call(f32[192,512]{1,0:T(8,128)S(1)} %select_select_fusion.own_ref, bf16[2048,512]{1,0:T(8,128)(2,1)S(1)} %copy-done, s32[8,256]{1,0:T(8,128)S(1)} %broadcast_in_dim.39.line_ref), custom_call_target="tpu_custom_call" | custom-call | tf_op jit(solution)/shard_map/exchange/pallas_call | solution.py:176
  49.9 0.0 copy-start.4
  49.9 1.0 copy-done.4
  50.8 0.0 copy-start.6
  50.8 0.7 copy-done.6
  51.6 0.0 copy-start.7
  51.6 0.7 copy-done.7
  52.3 20.5 %solve.1.coeffs_ref = f32[192,512]{1,0:T(8,128)} custom-call(f32[192,256]{1,0:T(8,128)} %copy-done.7, f32[192,512]{1,0:T(8,128)} %copy-done.6), custom_call_target="tpu_custom_call" | custom-call | tf_op jit(solution)/shard_map/solve/pallas_call | solution.py:245
  72.8 0.0 copy-done.2
  72.8 1.0 copy-done.1
  73.8 1.2 %copy-done.3 = bf16[1024,512]{1,0:T(8,128)(2,1)S(1)} copy-done((bf16[1024,512]{1,0:T(8,128)(2,1)S(1)}, bf16[1024,512]{1,0:T(8,128)(2,1)}, u32[]{:S(2)}) %copy-start.3) | copy-done | bytes 1048600
  75.0 1.2 %copy-done.5 = bf16[2048,256]{1,0:T(8,128)(2,1)S(1)} copy-done((bf16[2048,256]{1,0:T(8,128)(2,1)S(1)}, bf16[2048,256]{1,0:T(8,128)(2,1)}, u32[]{:S(2)}) %copy-start.5) | copy-done | bytes 1048600
  76.2 29.7 %reduce_error.1 = (bf16[2048,512]{1,0:T(8,128)(2,1)S(1)}, f32[32,2048]{1,0:T(8,128)S(1)}) custom-call(bf16[2048,512]{1,0:T(8,128)(2,1)} %weight_ref.3, bf16[2048,256]{1,0:T(8,128)(2,1)S(1)} %copy-done.5, f32[192,512]{1,0:T(8,128)S(1)} %copy-done.1, s32[2048,128]{1,0:T(8,128)S(1)} %copy-done.2, bf16[16,2048]{1,0:T(8,128)(2,1)S(1)} %broadcast_in_dim.40.limit_ref, ...), custom_call_target="tpu_custom_call" | custom-call | tf_op jit(solution)/shard_map/reduce_error/pallas_call | solution.py:432
  105.9 1.3 %copy.10 = bf16[2048,512]{1,0:T(8,128)(2,1)} copy(bf16[2048,512]{1,0:T(8,128)(2,1)S(1)} %get-tuple-element.16) | data formatting | bytes 4194304
  107.3 0.7 copy.11
  (9 shorter events, 0.0 us)
Async XLA Ops:
  2.9 6.5 %copy-start = (bf16[2048,512]{1,0:T(8,128)(2,1)S(1)}, bf16[2048,512]{1,0:T(8,128)(2,1)}, u32[]{:S(2)}) copy-start(bf16[2048,512]{1,0:T(8,128)(2,1)} %weight_ref.3) | copy-start | bytes 6291460
  8.2 64.5 %copy-start.2 = (s32[2048,128]{1,0:T(8,128)S(1)}, s32[2048,128]{1,0:T(8,128)}, u32[]{:S(2)}) copy-start(s32[2048,128]{1,0:T(8,128)} %mask_ref.1) | copy-start | bytes 3145732
  49.9 1.0 copy-start.4
  50.8 0.7 copy-start.6
  51.6 0.7 copy-start.7
  72.8 1.0 copy-start.1
  73.8 1.2 %copy-start.3 = (bf16[1024,512]{1,0:T(8,128)(2,1)S(1)}, bf16[1024,512]{1,0:T(8,128)(2,1)}, u32[]{:S(2)}) copy-start(bf16[1024,512]{1,0:T(8,128)(2,1)} %features_ref.1) | copy-start | bytes 3145732
  75.0 1.2 %copy-start.5 = (bf16[2048,256]{1,0:T(8,128)(2,1)S(1)}, bf16[2048,256]{1,0:T(8,128)(2,1)}, u32[]{:S(2)}) copy-start(bf16[2048,256]{1,0:T(8,128)(2,1)} %copy-done.4) | copy-start | bytes 3145732

commit v4 on v3

--- a/solution.py
+++ b/solution.py
@@ -208,34 +208,143 @@
     )(own_rows, weight, line)
 
 
+def gather_kernel(offset_ref, selected_ref, inverse_ref, own_ref, line_ref, sems):
+    steps, width = selected_ref.shape
+    height = inverse_ref.shape[0]
+    lane = lax.broadcasted_iota(jnp.int32, line_ref.shape, 1)
+
+    def wanted(k):
+        return selected_ref[k // width, lax.rem(k, width)]
+
+    def row_copy(k, spot):
+        return pltpu.make_async_copy(inverse_ref.at[pl.ds(spot, 1)], own_ref.at[pl.ds(k, 1)], sems.at[k])
+
+    def start(k, line):
+        picked = wanted(k)
+        spot = picked - offset_ref[0]
+        inside = (spot >= 0) & (spot < height)
+
+        @pl.when(inside)
+        def _():
+            row_copy(k, spot).start()
+
+        @pl.when(jnp.logical_not(inside))
+        def _():
+            own_ref[pl.ds(k, 1), :] = jnp.zeros((1, own_ref.shape[1]), jnp.float32)
+
+        return jnp.where(lane == k, picked, line)
+
+    line_ref[...] = lax.fori_loop(0, steps * width, start, jnp.full(line_ref.shape, -1, jnp.int32))
+
+    def finish(k, carry):
+        spot = wanted(k) - offset_ref[0]
+
+        @pl.when((spot >= 0) & (spot < height))
+        def _():
+            row_copy(k, spot).wait()
+
+        return carry
+
+    lax.fori_loop(0, steps * width, finish, 0)
+
+
+def gather(offset, selected, inverse):
+    count = selected.size
+    smem = pl.BlockSpec(memory_space=pltpu.SMEM)
+    vmem = pl.BlockSpec(memory_space=pltpu.VMEM)
+    return pl.pallas_call(
+        gather_kernel,
+        out_shape=(
+            jax.ShapeDtypeStruct((count, inverse.shape[1]), jnp.float32),
+            jax.ShapeDtypeStruct((8, LANES), jnp.int32),
+        ),
+        in_specs=[smem, smem, pl.BlockSpec(memory_space=pl.ANY)],
+        out_specs=(vmem, vmem),
+        scratch_shapes=[pltpu.SemaphoreType.DMA((count,))],
+        name="gather",
+    )(offset, selected, inverse)
+
+
+def invert(state):
+    count = state.shape[0]
+    size = 8
+    lane = lax.broadcasted_iota(jnp.int32, (size, BLK), 1)
+    line = lax.broadcasted_iota(jnp.int32, (size, BLK), 0)
+
+    def column(tile, at):
+        return jnp.take_along_axis(tile, jnp.full((size, BLK), at, jnp.int32), axis=1)
+
+    def row(tile, k):
+        return jnp.broadcast_to(tile[k : k + 1, :], tile.shape)
+
+    def lines_of(block):
+        return pl.ds(aligned(block * size, size), size)
+
+    def spot_of(block):
+        half = block * size // BLK
+        return half, block * size - half * BLK
+
+    def tile_of(half):
+        return pl.ds(aligned(half * BLK, BLK), BLK)
+
+    def blend(tile, columns, rows):
+        for j in range(0, size, 2):
+            tile = tile - (columns[j] * rows[j] + columns[j + 1] * rows[j + 1])
+        return tile
+
+    def columns_of(tile, at):
+        return [column(tile, at + j) for j in range(size)]
+
+    def step(block, pivot):
+        pivot = list(pivot)
+        for k in range(size):
+            scale = 1.0 / row(pivot[k], k)
+            lead = pivot[k]
+            for j in range(size):
+                if j != k:
+                    scaled = row(pivot[j], k) * scale
+                    pivot[j] = jnp.where(line == k, scaled, pivot[j] - lead * scaled)
+            pivot[k] = jnp.where(line == k, scale, -lead * scale)
+        half, at = spot_of(block)
+        inside = (lane >= at) & (lane < at + size)
+        unit = jnp.where(lane - at == line, 1.0, 0.0)
+        fresh, rows, here = [], [], []
+        for q in range(state.shape[1] // BLK):
+            mine = inside & (half == q)
+            here.append(mine)
+            tile = jnp.where(mine, unit, state[lines_of(block), q * BLK : (q + 1) * BLK])
+            parts = [pivot[j] * row(tile, j) for j in range(size)]
+            while len(parts) > 1:
+                parts = [parts[i] + parts[i + 1] for i in range(0, len(parts), 2)]
+            fresh.append(parts[0])
+            rows.append([row(parts[0], j) for j in range(size)])
+        following = jnp.minimum(block + 1, count // size - 1)
+        next_half, next_at = spot_of(following)
+        ahead = columns_of(state[lines_of(following), tile_of(half)], at)
+        next_fresh = jnp.where(next_half == 0, fresh[0], fresh[1])
+        next_tile = jnp.where(inside & (half == next_half), 0.0, state[lines_of(following), tile_of(next_half)])
+        next_tile = blend(next_tile, ahead, [row(next_fresh, j) for j in range(size)])
+        next_pivot = columns_of(next_tile, next_at)
+        for i in range(count // size):
+            group = slice(i * size, (i + 1) * size)
+            columns = columns_of(state[group, tile_of(half)], at)
+            for q in range(state.shape[1] // BLK):
+                lanes = slice(q * BLK, (q + 1) * BLK)
+                tile = jnp.where(here[q], 0.0, state[group, lanes])
+                state[group, lanes] = blend(tile, columns, rows[q])
+        for q in range(state.shape[1] // BLK):
+            state[lines_of(block), q * BLK : (q + 1) * BLK] = fresh[q]
+        return tuple(next_pivot)
+
+    first = tuple(columns_of(state[0:size, 0:BLK], 0))
+    return step, first
+
+
 def invert_kernel(square_ref, panel_ref, coeffs_ref, state):
     count = square_ref.shape[0]
-    side = 64
     state[...] = square_ref[...]
-    lane = lax.broadcasted_iota(jnp.int32, (side, BLK), 1)
-    line = lax.broadcasted_iota(jnp.int32, (side, BLK), 0)
-    for block in range(count // side):
-        lo = block * side
-        tile = state[lo : lo + side, (lo // BLK) * BLK : (lo // BLK) * BLK + BLK]
-        shift = lo % BLK
-        for k in range(side):
-            pivot_row = tile[k : k + 1, :]
-            column = jnp.take_along_axis(tile, jnp.full((side, BLK), k + shift, jnp.int32), axis=1)
-            scale = 1.0 / column[k : k + 1, :]
-            scaled = jnp.where(lane[0:1, :] == k + shift, scale, pivot_row * scale)
-            kept = jnp.where(lane == k + shift, 0.0, tile)
-            tile = jnp.where(line == k, scaled, kept - column * scaled)
-        inverse = tile[:, shift : shift + side]
-        strip = state[:, lo : lo + side]
-        lanes = lax.broadcasted_iota(jnp.int32, (side, LANES), 1)
-        inside = (lanes >= lo) & (lanes < lo + side)
-        unit = jnp.where(lanes - lo == lax.broadcasted_iota(jnp.int32, (side, LANES), 0), 1.0, 0.0)
-        right = jnp.where(inside, unit, state[lo : lo + side, :])
-        right = jnp.dot(inverse, right, precision=HIGHEST, preferred_element_type=jnp.float32)
-        all_lanes = lax.broadcasted_iota(jnp.int32, (count, LANES), 1)
-        cleared = jnp.where((all_lanes >= lo) & (all_lanes < lo + side), 0.0, state[...])
-        state[...] = cleared - jnp.dot(strip, right, precision=HIGHEST, preferred_element_type=jnp.float32)
-        state[lo : lo + side, :] = right
+    step, first = invert(state)
+    lax.fori_loop(0, count // 8, step, first)
     coeffs_ref[...] = jnp.dot(
         state[:, :count], panel_ref[...], precision=HIGHEST, preferred_element_type=jnp.float32
     )
@@ -465,19 +574,10 @@
 
 
 def local(weight, hess_inv, selected, block_mask, row_limits, calibration):
-    rows_local, cols_local = hess_inv.shape
+    rows_local = hess_inv.shape[0]
     out_local = weight.shape[0]
-    row_offset = lax.axis_index("rows") * rows_local
-    chosen = selected.reshape(-1)
-    count = chosen.shape[0]
-    row_place = chosen - row_offset
-    row_inside = (row_place >= 0) & (row_place < rows_local)
-    own_rows = jnp.where(
-        row_inside[:, None],
-        jnp.take(hess_inv, jnp.clip(row_place, 0, rows_local - 1), axis=0),
-        0.0,
-    )
-    line = jnp.broadcast_to(jnp.pad(chosen, (0, LANES - count), constant_values=-1)[None, :], (8, LANES))
+    row_offset = (lax.axis_index("rows") * rows_local).astype(jnp.int32).reshape(1)
+    own_rows, line = gather(row_offset, selected, hess_inv)
     square, panel, weight_cols = exchange(own_rows, weight, line)
     coeffs = solve(square, panel)
     limit = jnp.broadcast_to(row_limits[None, :], (16, out_local)).astype(jnp.bfloat16)

time: 108 us -> 148 us (1.37)
  Pallas kernels: 90.6 us -> 137 us
  local copies, waits for them, and re-layouts: 14 us -> 9.64 us
  other arithmetic: 2.61 us -> 0.7 us
    pallas_call x1, Pallas kernels: 20.5 us -> 55.5 us  [solve(): pl.pallas_call(invert_kernel, out_shape=jax.ShapeDtypeStruct(panel.shape,...]
    pallas_call x0 -> x1, Pallas kernels: none -> 11.5 us  [gather(): pl.pallas_call(gather_kernel, out_shape=(jax.ShapeDtypeStruct((count, inv...]
    gather x1 -> x0, local copies, waits for them, and re-layouts: 5.31 us -> none  [local(): jnp.take(hess_inv, jnp.clip(row_place, 0, rows_local - 1), axis=0)]
    unnamed x18 -> x22, local copies, waits for them, and re-layouts: 7.87 us -> 9.63 us
where the time goes in v4:
time: 148 us
  Pallas kernels  137 us (93%)
  local copies, waits for them, and re-layouts  9.64 us (7%)
    pallas_call x1, Pallas kernels, solve(): pl.pallas_call(invert_kernel, out_shape=jax.ShapeDtypeStruct(panel.shape,...  55.5 us
    pallas_call x1, Pallas kernels, exchange(): pl.pallas_call(exchange_kernel, out_shape=(jax.ShapeDtypeStruct((count, L...  40.2 us
    pallas_call x1, Pallas kernels, reduce_error(): pl.pallas_call(reduce_kernel, out_shape=(jax.ShapeDtypeStruct((rows, colu...  29.7 us
    pallas_call x1, Pallas kernels, gather(): pl.pallas_call(gather_kernel, out_shape=(jax.ShapeDtypeStruct((count, inv...  11.5 us
    unnamed x22, local copies, waits for them, and re-layouts  9.63 us

profile of v4, /device:TPU:1, one launch (start us, length us, event | category | flops | bytes accessed | tf_op | source)
XLA Modules:
  0.0 147.9 jit_solution(2789745836983039740)
XLA Ops:
  0.6 0.7 convert_element_type.3
  1.3 0.0 copy-start
  1.4 11.5 %gather.1 = (f32[192,512]{1,0:T(8,128)}, s32[8,256]{1,0:T(8,128)}) custom-call(s32[1]{0:T(128)} %bitcast.offset_ref, s32[3,64]{1,0:T(4,128)} %selected_ref.1, f32[4096,512]{1,0:T(8,128)} %inverse_ref.1), custom_call_target="tpu_custom_call" | custom-call | tf_op jit(solution)/shard_map/gather/pallas_call | solution.py:255
  12.8 0.0 copy-start.2
  12.8 0.0 copy-done
  12.9 0.0 copy-start.6
  12.9 1.1 copy-done.6
  13.9 0.0 copy-start.9
  13.9 0.7 copy-done.9
  14.6 40.2 %exchange.1 = (f32[192,256]{1,0:T(8,128)S(1)}, f32[192,512]{1,0:T(8,128)S(1)}, bf16[2048,256]{1,0:T(8,128)(2,1)S(1)}) custom-call(f32[192,512]{1,0:T(8,128)S(1)} %copy-done.6, bf16[2048,512]{1,0:T(8,128)(2,1)S(1)} %copy-done, s32[8,256]{1,0:T(8,128)S(1)} %copy-done.9), custom_call_target="tpu_custom_call" | custom-call | tf_op jit(solution)/shard_map/exchange/pallas_call | solution.py:176
  54.9 0.0 copy-start.4
  54.9 1.0 copy-done.4
  55.9 0.0 copy-start.7
  55.9 0.7 copy-done.7
  56.6 0.0 copy-start.8
  56.6 0.7 copy-done.8
  57.3 55.5 %solve.1.coeffs_ref = f32[192,512]{1,0:T(8,128)} custom-call(f32[192,256]{1,0:T(8,128)} %copy-done.8, f32[192,512]{1,0:T(8,128)} %copy-done.7), custom_call_target="tpu_custom_call" | custom-call | tf_op jit(solution)/shard_map/solve/pallas_call | solution.py:354
  112.7 0.0 copy-done.2
  112.7 1.0 copy-done.1
  113.7 1.2 copy-done.3
  115.0 1.2 copy-done.5
  116.2 29.7 %reduce_error.1 = (bf16[2048,512]{1,0:T(8,128)(2,1)S(1)}, f32[32,2048]{1,0:T(8,128)S(1)}) custom-call(bf16[2048,512]{1,0:T(8,128)(2,1)} %weight_ref.3, bf16[2048,256]{1,0:T(8,128)(2,1)S(1)} %copy-done.5, f32[192,512]{1,0:T(8,128)S(1)} %copy-done.1, s32[2048,128]{1,0:T(8,128)S(1)} %copy-done.2, bf16[16,2048]{1,0:T(8,128)(2,1)S(1)} %broadcast_in_dim.2.limit_ref, ...), custom_call_target="tpu_custom_call" | custom-call | tf_op jit(solution)/shard_map/reduce_error/pallas_call | solution.py:541
  145.9 1.3 copy.10
  147.2 0.7 copy.11
  (4 shorter events, 0.0 us)
Async XLA Ops:
  1.3 11.5 %copy-start = (bf16[2048,512]{1,0:T(8,128)(2,1)S(1)}, bf16[2048,512]{1,0:T(8,128)(2,1)}, u32[]{:S(2)}) copy-start(bf16[2048,512]{1,0:T(8,128)(2,1)} %weight_ref.3) | copy-start | bytes 6291460
  12.8 99.9 %copy-start.2 = (s32[2048,128]{1,0:T(8,128)S(1)}, s32[2048,128]{1,0:T(8,128)}, u32[]{:S(2)}) copy-start(s32[2048,128]{1,0:T(8,128)} %mask_ref.1) | copy-start | bytes 3145732
  12.9 1.1 copy-start.6
  13.9 0.7 copy-start.9
  54.9 1.0 copy-start.4
  55.9 0.7 copy-start.7
  56.6 0.7 copy-start.8
  112.7 1.0 copy-start.1
  113.7 1.2 copy-start.3
  115.0 1.2 copy-start.5

commit v5 on v2

v5 whole, which is shorter than its diff:
```python
import functools

import jax
import jax.numpy as jnp
from jax import lax
from jax.experimental import pallas as pl
from jax.experimental.pallas import tpu as pltpu
from jax.sharding import PartitionSpec as P

BLK = 128
LANES = 256
MESH = pl.DeviceIdType.MESH
HIGHEST = lax.Precision.HIGHEST


def aligned(value, factor):
    return pl.multiple_of(value, factor)


def place():
    row = lax.axis_index("rows")
    col = lax.axis_index("cols")
    core = lax.rem(col, 2)
    z = lax.rem(col // 2, 4)
    y = col // 8
    partner = (row, col + 1 - 2 * core)
    axes = {
        "x": (row, lambda j: (j, col)),
        "y": (y, lambda j: (row, (j * 4 + z) * 2 + core)),
        "z": (z, lambda j: (row, (y * 4 + j) * 2 + core)),
    }
    return core, partner, axes


def enter(partner, axes):
    barrier = pltpu.get_barrier_semaphore()
    pl.semaphore_signal(barrier, inc=1, device_id=partner, device_id_type=MESH)
    for index, device in axes.values():
        for step in (1, 2, 3):
            pl.semaphore_signal(
                barrier, inc=1, device_id=device(lax.rem(index + step, 4)), device_id_type=MESH
            )
    pl.semaphore_wait(barrier, 1 + 3 * len(axes))


def gather_kernel(offset_ref, selected_ref, values_ref, inverse_ref, own_ref, line_ref, sem):
    steps, width = selected_ref.shape
    height = inverse_ref.shape[0]
    for step in range(steps):

        @pl.loop(0, width, unroll=16)
        def _(k):
            spot = jnp.clip(selected_ref[step, k] - offset_ref[0], 0, height - 1)
            pltpu.make_async_copy(
                inverse_ref.at[pl.ds(spot, 1)], own_ref.at[pl.ds(step * width + k, 1)], sem
            ).start()

    line_ref[...] = jnp.full(line_ref.shape, -1, jnp.int32)
    for step in range(steps):
        line_ref[0:1, step * width : (step + 1) * width] = values_ref[step : step + 1, :]
    pltpu.make_async_copy(inverse_ref.at[pl.ds(0, own_ref.shape[0])], own_ref, sem).wait()


def gather(offset, selected, inverse):
    count = selected.size
    smem = pl.BlockSpec(memory_space=pltpu.SMEM)
    vmem = pl.BlockSpec(memory_space=pltpu.VMEM)
    return pl.pallas_call(
        gather_kernel,
        out_shape=(
            jax.ShapeDtypeStruct((count, inverse.shape[1]), jnp.float32),
            jax.ShapeDtypeStruct((8, LANES), jnp.int32),
        ),
        in_specs=[smem, smem, vmem, pl.BlockSpec(memory_space=pl.ANY)],
        out_specs=(vmem, vmem),
        scratch_shapes=[pltpu.SemaphoreType.DMA],
        name="gather",
    )(offset, selected, selected, inverse)


def invert(state, right, between):
    count, width = state.shape
    size, side = 8, 64
    blocks = side // size
    lane = lax.broadcasted_iota(jnp.int32, (size, BLK), 1)
    line = lax.broadcasted_iota(jnp.int32, (size, BLK), 0)

    def column(tile, at):
        return jnp.take_along_axis(tile, jnp.full((size, BLK), at, jnp.int32), axis=1)

    def row(tile, k):
        return jnp.broadcast_to(tile[k : k + 1, :], tile.shape)

    def fold(parts):
        while len(parts) > 1:
            parts = [parts[i] + parts[i + 1] for i in range(0, len(parts), 2)]
        return parts[0]

    def step(t, carry):
        half = t // 2
        shift = (t - half * 2) * side
        lanes = pl.ds(aligned(half * BLK, BLK), BLK)
        groups = [state[pl.ds(aligned(t * side + i * size, size), size), lanes] for i in range(blocks)]
        for b in range(blocks):
            at = shift + b * size
            pivot = [column(groups[b], at + j) for j in range(size)]
            for k in range(size):
                scale = 1.0 / row(pivot[k], k)
                lead = pivot[k]
                for j in range(size):
                    if j != k:
                        scaled = row(pivot[j], k) * scale
                        pivot[j] = jnp.where(line == k, scaled, pivot[j] - lead * scaled)
                pivot[k] = jnp.where(line == k, scale, -lead * scale)
            inside = (lane >= at) & (lane < at + size)
            tile = jnp.where(inside, jnp.where(lane - at == line, 1.0, 0.0), groups[b])
            fresh = fold([pivot[j] * row(tile, j) for j in range(size)])
            rows = [row(fresh, j) for j in range(size)]
            order = [(b + 1 + i) % blocks for i in range(blocks - 1)]
            for i in order:
                change = fold([column(groups[i], at + j) * rows[j] for j in range(size)])
                groups[i] = jnp.where(inside, 0.0, groups[i]) - change
            groups[b] = fresh
        mine = (lane >= shift) & (lane < shift + side)
        block = jnp.concatenate([jnp.where(mine, group, 0.0) for group in groups], axis=0)
        own = pl.ds(aligned(shift, side), side)
        lines = pl.ds(aligned(t * side, side), side)
        wide = lax.broadcasted_iota(jnp.int32, (side, width), 1) - t * side
        unit = jnp.where(wide == lax.broadcasted_iota(jnp.int32, (side, width), 0), 1.0, 0.0)
        right[...] = jnp.zeros(right.shape, jnp.float32)
        right[own, :] = jnp.where((wide >= 0) & (wide < side), unit, state[lines, :])
        solved = jnp.dot(block, right[...], precision=HIGHEST, preferred_element_type=jnp.float32)
        right[own, :] = solved
        tall = lax.broadcasted_iota(jnp.int32, (count, BLK), 1)
        strip = jnp.where((tall >= shift) & (tall < shift + side), state[:, lanes], 0.0)
        spans = lax.broadcasted_iota(jnp.int32, (count, width), 1) - t * side
        cleared = jnp.where((spans >= 0) & (spans < side), 0.0, state[...])
        state[...] = cleared - jnp.dot(strip, right[...], precision=HIGHEST, preferred_element_type=jnp.float32)
        state[lines, :] = solved
        between(t)
        return carry

    lax.fori_loop(0, count // side, step, 0)


def prune_kernel(
    own_ref, line_ref, limit_ref, weight_any, mask_any, features_any, pruned_any, error_ref,
    weight_ref, mask_ref, features_ref, kept, limits,
    own_rows, square_part, half_rx, half, z_rx, z_sum, y_rx, y_sum, x_rx, square_ref, state, right,
    panel_rx, panel_ref, weight_part, weight_rx, weight_half, first_rx, first_sum, second_rx, chosen_ref,
    high, low, features_rx, own_diff, sent_diff, diff_rx, pruned_ref, part, forward_rx, forward, ring_rx,
    sums, sums_wide, small_forward_rx, small_forward, small_rx, final,
    send_sem, recv_sem, local_sem, pruned_sem,
    *, height,
):
    core, partner, axes = place()
    rows, columns = weight_ref.shape
    col_offset = lax.axis_index("cols") * columns
    count = own_ref.shape[0]
    half_rows = count // 2
    quarter = half_rows // 4
    share = rows // 2
    chunks = part.shape[0]
    chunk = share // chunks
    blocks = columns // BLK
    f32, bf16 = jnp.float32, jnp.bfloat16
    started = []

    loads = [
        pltpu.make_async_copy(src, dst, local_sem.at[i])
        for i, (src, dst) in enumerate(
            ((weight_any, weight_ref), (features_any, features_ref), (mask_any, mask_ref))
        )
    ]
    for load in loads:
        load.start()

    def remote(src, dst, stage, slot, device):
        return pltpu.make_async_remote_copy(
            src_ref=src, dst_ref=dst, send_sem=send_sem.at[stage, slot], recv_sem=recv_sem.at[stage, slot],
            device_id=device, device_id_type=MESH,
        )

    def send(*args):
        copy = remote(*args)
        copy.start()
        started.append(copy)
        return copy

    def scatter(axis, src, base, piece, rx, stage):
        index, device = axes[axis]
        copies = []
        for step in (1, 2, 3):
            peer = lax.rem(index + step, 4)
            start = aligned(base + peer * piece, 8)
            copies.append(send(src.at[pl.ds(start, piece)], rx.at[step - 1], stage, step - 1, device(peer)))
        return copies

    def spread(axis, src, dst_of, stage):
        index, device = axes[axis]
        return [
            send(src, dst_of(step - 1), stage, step - 1, device(lax.rem(index + step, 4))) for step in (1, 2, 3)
        ]

    def arrive(copies):
        for copy in copies:
            copy.wait_recv()

    def total(own, rx):
        return own + rx[0] + rx[1] + rx[2]

    row_offset = lax.axis_index("rows") * height
    picked = line_ref[0:1, :count]
    owned = jnp.where((picked >= row_offset) & (picked < row_offset + height), 1.0, 0.0)
    first = lax.broadcasted_iota(jnp.int32, (16, count), 0) == 0
    owned = lax.dot_general(
        jnp.where(first, owned, 0.0).astype(bf16), jnp.ones((16, columns), bf16),
        (((0,), (0,)), ((), ())), preferred_element_type=f32,
    )
    own_rows[...] = jnp.where(owned > 0.5, own_ref[...], 0.0)
    lines = lax.broadcasted_iota(jnp.int32, (columns, LANES), 0) + col_offset
    onehot = jnp.where(lines == line_ref[0:1, :], 1.0, 0.0)
    square_part[...] = jnp.dot(own_rows[...], onehot, precision=HIGHEST, preferred_element_type=f32)
    loads[0].wait()
    weight_part[...] = jnp.dot(weight_ref[...], onehot.astype(bf16), preferred_element_type=f32).astype(bf16)

    enter(partner, axes)
    x, y, z = axes["x"][0], axes["y"][0], axes["z"][0]
    s1 = send(square_part.at[pl.ds(aligned((1 - core) * half_rows, 8), half_rows)], half_rx, 0, 0, partner)
    w1 = send(weight_part.at[pl.ds(aligned((1 - core) * share, 16), share)], weight_rx, 2, 0, partner)
    panel_piece = count // 4
    p1 = scatter("x", own_rows, 0, panel_piece, panel_rx, 1)
    loads[1].wait()
    features_copy = send(features_ref, features_rx, 18, 0, partner)
    s1.wait_recv()
    half[...] = square_part[pl.ds(aligned(core * half_rows, 8), half_rows), :] + half_rx[...]
    s2 = scatter("z", half, 0, quarter, z_rx, 3)
    w1.wait_recv()
    weight_half[...] = weight_part[pl.ds(aligned(core * share, 16), share), :] + weight_rx[...]
    span = share // 2
    piece = span // 4
    small = piece // 4
    wa = scatter("y", weight_half, 0, piece, first_rx.at[0], 6)
    wb = scatter("z", weight_half, span, piece, first_rx.at[1], 7)

    loads[2].wait()
    limits[...] = jnp.broadcast_to(limit_ref[0:1, :].astype(f32), limits.shape).astype(bf16)
    place_line = lax.broadcasted_iota(jnp.int32, (BLK, columns), 0)
    block = lax.axis_index("cols") * blocks + lax.broadcasted_iota(jnp.int32, (BLK, columns), 1) // BLK
    before = jnp.where(place_line <= block, 1.0, 0.0).astype(bf16)
    here = jnp.where(place_line == block, 1.0, 0.0).astype(bf16)
    lead = jnp.where(lax.broadcasted_iota(jnp.int32, (16, columns), 0) == 0, 1.0, 0.0).astype(bf16)

    def keep(low_chunk, high_chunk):
        @pl.loop(low_chunk, high_chunk)
        def _(i):
            spots = pl.ds(aligned(i * chunk, chunk), chunk)
            mask = mask_ref[spots, :].astype(f32).astype(bf16)
            seen = jnp.dot(mask, before, preferred_element_type=f32)
            bit = jnp.dot(mask, here, preferred_element_type=f32)
            limit = lax.dot_general(
                limits[:, spots], lead, (((0,), (0,)), ((), ())), preferred_element_type=f32
            )
            kept[spots, :] = jnp.where(seen <= limit, bit, 0.0).astype(bf16)

    arrive(s2)
    z_sum[...] = total(half[pl.ds(aligned(z * quarter, 8), quarter), :], z_rx)
    s3 = spread("y", z_sum, lambda slot: y_rx.at[slot], 4)
    keep(0, chunks)
    arrive(s3)
    y_sum[...] = total(z_sum[...], y_rx)
    s4 = spread("x", y_sum, lambda slot: x_rx.at[slot], 5)
    arrive(wa)
    first_sum[0] = total(weight_half[pl.ds(aligned(y * piece, 16), piece), :], first_rx.at[0])
    wa = scatter("z", first_sum.at[0], 0, small, second_rx.at[0], 11)
    arrive(wb)
    first_sum[1] = total(weight_half[pl.ds(aligned(span + z * piece, 16), piece), :], first_rx.at[1])
    wb = scatter("y", first_sum.at[1], 0, small, second_rx.at[1], 12)
    arrive(s4)
    mine = pl.ds(aligned(core * half_rows + z * quarter, 8), quarter)
    square_ref[mine, :] = total(y_sum[...], x_rx)
    s5 = spread("z", square_ref.at[mine], lambda slot: square_ref.at[mine], 8)
    arrive(p1)
    own_panel = pl.ds(aligned(x * panel_piece, 8), panel_piece)
    panel_ref[own_panel, :] = total(own_rows[own_panel, :], panel_rx)
    p2 = spread("x", panel_ref.at[own_panel], lambda slot: panel_ref.at[own_panel], 9)
    arrive(wa)
    base_a = core * share + y * piece
    base_b = core * share + span + z * piece
    slice_a = pl.ds(aligned(base_a + z * small, 16), small)
    slice_b = pl.ds(aligned(base_b + y * small, 16), small)
    chosen_ref[slice_a, :] = total(first_sum[0, pl.ds(aligned(z * small, 16), small), :], second_rx.at[0])
    wa = spread("z", chosen_ref.at[slice_a], lambda slot: chosen_ref.at[slice_a], 13)
    arrive(wb)
    chosen_ref[slice_b, :] = total(first_sum[1, pl.ds(aligned(y * small, 16), small), :], second_rx.at[1])
    wb = spread("y", chosen_ref.at[slice_b], lambda slot: chosen_ref.at[slice_b], 14)
    arrive(s5)
    own_half = pl.ds(aligned(core * half_rows, 8), half_rows)
    s6 = send(square_ref.at[own_half], square_ref.at[own_half], 10, 0, partner)
    keep(chunks, 2 * chunks)
    arrive(wa)
    piece_a = pl.ds(aligned(base_a, 16), piece)
    wa = spread("y", chosen_ref.at[piece_a], lambda slot: chosen_ref.at[piece_a], 15)
    arrive(wb)
    piece_b = pl.ds(aligned(base_b, 16), piece)
    wb = spread("z", chosen_ref.at[piece_b], lambda slot: chosen_ref.at[piece_b], 16)
    s6.wait_recv()
    own_share = pl.ds(aligned(core * share, 16), share)
    w6 = remote(chosen_ref.at[own_share], chosen_ref.at[own_share], 17, 0, partner)

    def between(t):
        @pl.when(t == 1)
        def _():
            arrive(wa)
            arrive(wb)
            w6.start()

    state[...] = square_ref[...]
    invert(state, right, between)
    arrive(p2)
    coeffs = jnp.dot(state[:, :count], panel_ref[...], precision=HIGHEST, preferred_element_type=f32)
    high[...] = coeffs.astype(bf16)
    low[...] = (coeffs - high[...].astype(f32)).astype(bf16)
    w6.wait_recv()

    def pruned_copy(i):
        spots = pl.ds(aligned(i * chunk, chunk), chunk)
        return pltpu.make_async_copy(pruned_ref.at[spots], pruned_any.at[spots], pruned_sem.at[i])

    def differ(index):
        spots = pl.ds(aligned(index * chunk, chunk), chunk)
        chosen = chosen_ref[spots, :][:, :count]
        change = jnp.dot(chosen, high[...], preferred_element_type=f32)
        change += jnp.dot(chosen, low[...], preferred_element_type=f32)
        wide = weight_ref[spots, :].astype(f32)
        masked = (wide - change) * kept[spots, :].astype(f32)
        pruned_ref[spots, :] = masked.astype(bf16)
        return (wide - masked).astype(bf16)

    diff_copies = {}

    def prepare(k):
        spots = slice(k * chunk, (k + 1) * chunk)
        sent_diff[spots, :] = differ((1 - core) * chunks + k)
        diff_copies[k] = send(sent_diff.at[spots], diff_rx.at[spots], 19, k, partner)
        own_diff[spots, :] = differ(core * chunks + k)

    token_blocks = part.shape[1]

    def multiply(k):
        spots = slice(k * chunk, (k + 1) * chunk)
        tokens = features_ref.shape[0] // token_blocks

        @pl.loop(0, token_blocks)
        def _(t):
            words = pl.ds(aligned(t * tokens, tokens), tokens)
            product = lax.dot_general(
                features_ref[words, :], own_diff[spots, :], (((1,), (1,)), ((), ())), preferred_element_type=f32
            )
            product += lax.dot_general(
                features_rx[words, :], diff_rx[spots, :], (((1,), (1,)), ((), ())), preferred_element_type=f32
            )
            part[k, t] = product.astype(bf16).reshape(part.shape[2:])

    def ring(axis, sent, value, extent, through_rx, through, rx, stage):
        index, device = axes[axis]
        right_one, left_one, across = lax.rem(index + 1, 4), lax.rem(index + 3, 4), lax.rem(index + 2, 4)
        lo, hi = pl.ds(0, extent // 2), pl.ds(extent // 2, extent // 2)
        a = send(sent(across).at[lo], through_rx.at[0], stage, 0, device(right_one))
        b = send(sent(across).at[hi], through_rx.at[1], stage, 1, device(left_one))
        c = send(sent(right_one).at[hi], rx.at[0, hi], stage, 2, device(right_one))
        d = send(sent(left_one).at[lo], rx.at[1, lo], stage, 3, device(left_one))
        later = []

        def pass_on():
            a.wait_recv()
            through[0] = (value(right_one, lo) + through_rx[0].astype(f32)).astype(bf16)
            later.append(send(through.at[0], rx.at[0, lo], stage, 4, device(right_one)))
            b.wait_recv()
            through[1] = (value(left_one, hi) + through_rx[1].astype(f32)).astype(bf16)
            later.append(send(through.at[1], rx.at[1, hi], stage, 5, device(left_one)))

        def finish():
            for copy in (c, d, *later):
                copy.wait_recv()
            return value(index, pl.ds(0, extent)) + rx[0].astype(f32) + rx[1].astype(f32)

        return pass_on, finish

    order = [k for pair in zip(range(chunks // 2), range(chunks // 2, chunks)) for k in pair]
    rings = {}

    def reduce_first(k):
        if k == order[0]:
            features_copy.wait_recv()
        diff_copies[k].wait_recv()
        multiply(k)
        if k < chunks // 2:
            axis = "y"
            sent = functools.partial(lambda k, j: part.at[k, j], k)
        else:
            axis = "z"
            sent = functools.partial(lambda k, j: part.at[k, :, j], k)
        value = functools.partial(lambda sent, j, which: sent(j).at[which][...].astype(f32), sent)
        rings[k] = ring(axis, sent, value, 4, forward_rx.at[k], forward.at[k], ring_rx.at[k], 20 + k)

    prepare(order[0])
    prepare(order[1])
    for n, k in enumerate(order):
        reduce_first(k)
        if n + 2 < chunks:
            prepare(order[n + 2])
    for k in range(2 * chunks):
        pruned_copy(k).start()
    for k in order:
        rings[k][0]()
    again = {}
    for k in order:
        value_sum = rings[k][1]()
        sums_wide[k] = value_sum
        sums[k] = value_sum.astype(bf16)
        axis = "z" if k < chunks // 2 else "y"
        sent = functools.partial(lambda k, j: sums.at[k, j], k)
        value = functools.partial(lambda k, j, which: sums_wide[k, j, which, :], k)
        again[k] = ring(
            axis, sent, value, 64, small_forward_rx.at[k], small_forward.at[k], small_rx.at[k], 20 + chunks + k
        )
    for k in order:
        again[k][0]()
    tokens = error_ref.shape[0]
    last = []
    for k in order:
        final[k] = again[k][1]()
        lanes = pl.ds(aligned(core * share + k * chunk, chunk), chunk)
        last.append(
            send(
                final.at[k, pl.ds(aligned((1 - core) * tokens, tokens), tokens)],
                error_ref.at[:, lanes], 20 + 2 * chunks, k, partner,
            )
        )
        error_ref[:, lanes] = final[k, pl.ds(aligned(core * tokens, tokens), tokens), :]
    for k in range(2 * chunks):
        pruned_copy(k).wait()
    arrive(last)
    w6.wait_send()
    for copy in started:
        copy.wait_send()


def prune(own_rows, line, limit, weight, mask, features, height):
    count, columns = own_rows.shape
    rows = weight.shape[0]
    tokens = features.shape[0]
    f32, bf16 = jnp.float32, jnp.bfloat16
    half, quarter = count // 2, count // 8
    share, chunks = rows // 2, 4
    piece = share // 8
    small = piece // 4
    chunk = share // chunks
    vmem = pl.BlockSpec(memory_space=pltpu.VMEM)
    hbm = pl.BlockSpec(memory_space=pl.ANY)
    stages = 21 + 2 * chunks
    return pl.pallas_call(
        functools.partial(prune_kernel, height=height),
        out_shape=(
            jax.ShapeDtypeStruct((rows, columns), bf16),
            jax.ShapeDtypeStruct((tokens // 32, rows), f32),
        ),
        in_specs=[vmem, vmem, vmem, hbm, hbm, hbm],
        out_specs=(hbm, vmem),
        scratch_shapes=[
            pltpu.VMEM((rows, columns), bf16),
            pltpu.VMEM(mask.shape, jnp.int32),
            pltpu.VMEM(features.shape, bf16),
            pltpu.VMEM((rows, columns), bf16),
            pltpu.VMEM((16, rows), bf16),
            pltpu.VMEM((count, columns), f32),
            pltpu.VMEM((count, LANES), f32),
            pltpu.VMEM((half, LANES), f32),
            pltpu.VMEM((half, LANES), f32),
            pltpu.VMEM((3, quarter, LANES), f32),
            pltpu.VMEM((quarter, LANES), f32),
            pltpu.VMEM((3, quarter, LANES), f32),
            pltpu.VMEM((quarter, LANES), f32),
            pltpu.VMEM((3, quarter, LANES), f32),
            pltpu.VMEM((count, LANES), f32),
            pltpu.VMEM((count, LANES), f32),
            pltpu.VMEM((BLK, LANES), f32),
            pltpu.VMEM((3, count // 4, columns), f32),
            pltpu.VMEM((count, columns), f32),
            pltpu.VMEM((rows, LANES), bf16),
            pltpu.VMEM((share, LANES), bf16),
            pltpu.VMEM((share, LANES), bf16),
            pltpu.VMEM((2, 3, piece, LANES), bf16),
            pltpu.VMEM((2, piece, LANES), bf16),
            pltpu.VMEM((2, 3, small, LANES), bf16),
            pltpu.VMEM((rows, LANES), bf16),
            pltpu.VMEM((count, columns), bf16),
            pltpu.VMEM((count, columns), bf16),
            pltpu.VMEM(features.shape, bf16),
            pltpu.VMEM((share, columns), bf16),
            pltpu.VMEM((share, columns), bf16),
            pltpu.VMEM((share, columns), bf16),
            pltpu.VMEM((rows, columns), bf16),
            pltpu.VMEM((chunks, 4, 4, 64, chunk), bf16),
            pltpu.VMEM((chunks, 2, 2, 64, chunk), bf16),
            pltpu.VMEM((chunks, 2, 2, 64, chunk), bf16),
            pltpu.VMEM((chunks, 2, 4, 64, chunk), bf16),
            pltpu.VMEM((chunks, 4, 64, chunk), bf16),
            pltpu.VMEM((chunks, 4, 64, chunk), f32),
            pltpu.VMEM((chunks, 2, 32, chunk), bf16),
            pltpu.VMEM((chunks, 2, 32, chunk), bf16),
            pltpu.VMEM((chunks, 2, 64, chunk), bf16),
            pltpu.VMEM((chunks, 64, chunk), f32),
            pltpu.SemaphoreType.DMA((stages, 6)),
            pltpu.SemaphoreType.DMA((stages, 6)),
            pltpu.SemaphoreType.DMA((3,)),
            pltpu.SemaphoreType.DMA((2 * chunks,)),
        ],
        compiler_params=pltpu.CompilerParams(
            collective_id=0, has_side_effects=True, vmem_limit_bytes=56 << 20
        ),
        name="prune",
    )(own_rows, line, limit, weight, mask, features)


def local(weight, hess_inv, selected, block_mask, row_limits, calibration):
    rows_local = hess_inv.shape[0]
    row_offset = (lax.axis_index("rows") * rows_local).astype(jnp.int32).reshape(1)
    own_rows, line = gather(row_offset, selected, hess_inv)
    pruned, error = prune(
        own_rows, line, row_limits.reshape(1, -1), weight, block_mask, calibration, rows_local
    )
    return (pruned, error.T)


def solution(mesh):
    placed = (
        P("rows", "cols"),
        P("rows", "cols"),
        P(),
        P("rows", None),
        P("rows"),
        P(None, "cols"),
    )
    return jax.shard_map(
        local,
        mesh=mesh,
        in_specs=placed,
        out_specs=(P("rows", "cols"), P("rows", "cols")),
        check_vma=False,
    )
```

time: 146 us -> 78.1 us (0.53)
  blocking collectives: 54.9 us -> 0 us
  local copies, waits for them, and re-layouts: 16.7 us -> 3.79 us
  Pallas kernels: 60.9 us -> 73.8 us
  other arithmetic: 6.41 us -> 0 us
  matrix products: 5.97 us -> 0 us
    all_to_all x1 -> x0, blocking collectives: 54.9 us -> none  [local(): lax.all_to_all(partial, 'cols', split_axis=0, concat_axis=0, tiled=True)]
    pallas_call x2, Pallas kernels: 60.9 us -> 73.8 us  [the longest x1 66.4 us: prune(): pl.pallas_call(functools.partial(prune_kernel, height=height), out_shape=...]
    dot_general x2 -> x0, matrix products: 5.97 us -> none  [the longest x1 3.56 us: local(): jnp.dot(weight_cols[:, :count].astype(jnp.float32), coeffs, precision=HIG...]
    mul x1 -> x0, local copies, waits for them, and re-layouts: 5.1 us -> none  [local(): refit.reshape(out_local, blocks_local, BLK)]
    gather x1 -> x0, local copies, waits for them, and re-layouts: 4.42 us -> none  [local(): jnp.take(hess_inv, jnp.clip(row_place, 0, rows_local - 1), axis=0)]
    another operation x1 -> x0, other arithmetic: 3.22 us -> none  [local(): running_count = jnp.cumsum(block_mask, axis=1)]
    reduce_sum x1 -> x0, other arithmetic: 1.47 us -> none  [local(): layer_error = jnp.sum(pieces.astype(jnp.float32), axis=0).T]
    unnamed x17 -> x4, local copies, waits for them, and re-layouts: 4.93 us -> 3.79 us
where the time goes in v5:
time: 78.1 us; the launch traced here: 78.3 us
  Pallas kernels  73.8 us (94%)
  local copies, waits for them, and re-layouts  3.79 us (5%)
    pallas_call x1, Pallas kernels, prune(): pl.pallas_call(functools.partial(prune_kernel, height=height), out_shape=...  66.4 us
    pallas_call x1, Pallas kernels, gather(): pl.pallas_call(gather_kernel, out_shape=(jax.ShapeDtypeStruct((count, inv...  7.41 us
    unnamed x4, local copies, waits for them, and re-layouts  3.79 us

profile of v5, /device:TPU:1, one launch (start us, length us, event | category | flops | bytes accessed | tf_op | source)
XLA Modules:
  0.0 78.3 jit_solution(12853762292263151386)
XLA Ops:
  0.6 7.4 %gather.1 = (f32[192,512]{1,0:T(8,128)}, s32[8,256]{1,0:T(8,128)}) custom-call(s32[1]{0:T(128)} %bitcast.offset_ref, s32[3,64]{1,0:T(4,128)} %values_ref.1, s32[3,64]{1,0:T(4,128)} %values_ref.1, f32[4096,512]{1,0:T(8,128)} %inverse_ref.1), custom_call_target="tpu_custom_call" | custom-call | tf_op jit(solution)/shard_map/gather/pallas_call | solution.py:68
  8.0 66.4 %prune.1 = (bf16[2048,512]{1,0:T(8,128)(2,1)}, f32[32,2048]{1,0:T(8,128)}) custom-call(f32[192,512]{1,0:T(8,128)} %get-tuple-element.6.own_ref, s32[8,256]{1,0:T(8,128)} %get-tuple-element.7.line_ref, s32[1,2048]{1,0:T(1,128)} %bitcast.4, bf16[2048,512]{1,0:T(8,128)(2,1)} %weight_any.1, s32[2048,128]{1,0:T(8,128)} %mask_any.1, bf16[1024,512]{1,0:T(8,128)(2,1)} %features_any.1), custom_call_target="tpu_custom_call" | custom-call | tf_op jit(solution)/shard_map/prune/pallas_call | solution.py:463
  74.5 0.0 copy-start
  74.5 3.1 %copy.10 = bf16[2048,512]{1,0:T(8,128)(2,1)} copy(bf16[2048,512]{1,0:T(8,128)(2,1)} %get-tuple-element.12) | data formatting | bytes 4194304
  77.6 0.0 copy-done
  77.6 0.7 copy.11
Async XLA Ops:
  74.5 3.1 %copy-start = (f32[32,2048]{1,0:T(8,128)S(1)}, f32[32,2048]{1,0:T(8,128)}, u32[]{:S(2)}) copy-start(f32[32,2048]{1,0:T(8,128)} %get-tuple-element.9) | copy-start | bytes 786436

commit v6 on v5

--- a/solution.py
+++ b/solution.py
@@ -46,19 +46,32 @@
 def gather_kernel(offset_ref, selected_ref, values_ref, inverse_ref, own_ref, line_ref, sem):
     steps, width = selected_ref.shape
     height = inverse_ref.shape[0]
+    def row_copy(spot, k):
+        return pltpu.make_async_copy(inverse_ref.at[pl.ds(spot, 1)], own_ref.at[pl.ds(k, 1)], sem)
+
+    owned = 0
     for step in range(steps):
 
-        @pl.loop(0, width, unroll=16)
-        def _(k):
-            spot = jnp.clip(selected_ref[step, k] - offset_ref[0], 0, height - 1)
-            pltpu.make_async_copy(
-                inverse_ref.at[pl.ds(spot, 1)], own_ref.at[pl.ds(step * width + k, 1)], sem
-            ).start()
-
+        def start(k, owned):
+            spot = selected_ref[step, k] - offset_ref[0]
+            inside = (spot >= 0) & (spot < height)
+
+            @pl.when(inside)
+            def _():
+                row_copy(spot, step * width + k).start()
+
+            return owned + jnp.where(inside, 1, 0)
+
+        owned = lax.fori_loop(0, width, start, owned, unroll=8)
     line_ref[...] = jnp.full(line_ref.shape, -1, jnp.int32)
     for step in range(steps):
         line_ref[0:1, step * width : (step + 1) * width] = values_ref[step : step + 1, :]
-    pltpu.make_async_copy(inverse_ref.at[pl.ds(0, own_ref.shape[0])], own_ref, sem).wait()
+
+    def finish(k, carry):
+        row_copy(0, 0).wait()
+        return carry
+
+    lax.fori_loop(0, owned, finish, 0)
 
 
 def gather(offset, selected, inverse):
@@ -85,8 +98,8 @@
     lane = lax.broadcasted_iota(jnp.int32, (size, BLK), 1)
     line = lax.broadcasted_iota(jnp.int32, (size, BLK), 0)
 
-    def column(tile, at):
-        return jnp.take_along_axis(tile, jnp.full((size, BLK), at, jnp.int32), axis=1)
+    def column(tile, k):
+        return jnp.broadcast_to(tile[:, k : k + 1], tile.shape)
 
     def row(tile, k):
         return jnp.broadcast_to(tile[k : k + 1, :], tile.shape)
@@ -100,9 +113,11 @@
         half = t // 2
         shift = (t - half * 2) * side
         lanes = pl.ds(aligned(half * BLK, BLK), BLK)
-        groups = [state[pl.ds(aligned(t * side + i * size, size), size), lanes] for i in range(blocks)]
+        lines = pl.ds(aligned(t * side, side), side)
+        moved = jnp.where(shift > 0, pltpu.roll(state[lines, lanes], side, 1), state[lines, lanes])
+        groups = [moved[i * size : (i + 1) * size] for i in range(blocks)]
         for b in range(blocks):
-            at = shift + b * size
+            at = b * size
             pivot = [column(groups[b], at + j) for j in range(size)]
             for k in range(size):
                 scale = 1.0 / row(pivot[k], k)
@@ -121,15 +136,15 @@
                 change = fold([column(groups[i], at + j) * rows[j] for j in range(size)])
                 groups[i] = jnp.where(inside, 0.0, groups[i]) - change
             groups[b] = fresh
-        mine = (lane >= shift) & (lane < shift + side)
-        block = jnp.concatenate([jnp.where(mine, group, 0.0) for group in groups], axis=0)
+        block = jnp.concatenate(groups, axis=0)[:, :side]
         own = pl.ds(aligned(shift, side), side)
-        lines = pl.ds(aligned(t * side, side), side)
         wide = lax.broadcasted_iota(jnp.int32, (side, width), 1) - t * side
         unit = jnp.where(wide == lax.broadcasted_iota(jnp.int32, (side, width), 0), 1.0, 0.0)
+        solved = jnp.dot(
+            block, jnp.where((wide >= 0) & (wide < side), unit, state[lines, :]),
+            precision=HIGHEST, preferred_element_type=jnp.float32,
+        )
         right[...] = jnp.zeros(right.shape, jnp.float32)
-        right[own, :] = jnp.where((wide >= 0) & (wide < side), unit, state[lines, :])
-        solved = jnp.dot(block, right[...], precision=HIGHEST, preferred_element_type=jnp.float32)
         right[own, :] = solved
         tall = lax.broadcasted_iota(jnp.int32, (count, BLK), 1)
         strip = jnp.where((tall >= shift) & (tall < shift + side), state[:, lanes], 0.0)
@@ -164,8 +179,6 @@
     chunk = share // chunks
     blocks = columns // BLK
     f32, bf16 = jnp.float32, jnp.bfloat16
-    started = []
-
     loads = [
         pltpu.make_async_copy(src, dst, local_sem.at[i])
         for i, (src, dst) in enumerate(
@@ -175,36 +188,35 @@
     for load in loads:
         load.start()
 
-    def remote(src, dst, stage, slot, device):
+    sent = {}
+
+    def remote(src, dst, arrival, group, device):
         return pltpu.make_async_remote_copy(
-            src_ref=src, dst_ref=dst, send_sem=send_sem.at[stage, slot], recv_sem=recv_sem.at[stage, slot],
+            src_ref=src, dst_ref=dst, send_sem=send_sem.at[group], recv_sem=recv_sem.at[arrival],
             device_id=device, device_id_type=MESH,
         )
 
-    def send(*args):
-        copy = remote(*args)
-        copy.start()
-        started.append(copy)
-        return copy
-
-    def scatter(axis, src, base, piece, rx, stage):
+    def send(src, dst, arrival, group, device):
+        remote(src, dst, arrival, group, device).start()
+        size = jnp.dtype(src.dtype).itemsize
+        for extent in src.shape:
+            size *= extent
+        sent[group] = sent.get(group, 0) + size
+
+    def arrive(view, arrival):
+        remote(view, view, arrival, 0, partner).wait_recv()
+
+    def scatter(axis, src, base, piece, rx, arrival, group):
         index, device = axes[axis]
-        copies = []
         for step in (1, 2, 3):
             peer = lax.rem(index + step, 4)
             start = aligned(base + peer * piece, 8)
-            copies.append(send(src.at[pl.ds(start, piece)], rx.at[step - 1], stage, step - 1, device(peer)))
-        return copies
-
-    def spread(axis, src, dst_of, stage):
+            send(src.at[pl.ds(start, piece)], rx.at[step - 1], arrival, group, device(peer))
+
+    def spread(axis, src, dst_of, arrival, group):
         index, device = axes[axis]
-        return [
-            send(src, dst_of(step - 1), stage, step - 1, device(lax.rem(index + step, 4))) for step in (1, 2, 3)
-        ]
-
-    def arrive(copies):
-        for copy in copies:
-            copy.wait_recv()
+        for step in (1, 2, 3):
+            send(src, dst_of(step - 1), arrival, group, device(lax.rem(index + step, 4)))
 
     def total(own, rx):
         return own + rx[0] + rx[1] + rx[2]
@@ -221,27 +233,27 @@
     lines = lax.broadcasted_iota(jnp.int32, (columns, LANES), 0) + col_offset
     onehot = jnp.where(lines == line_ref[0:1, :], 1.0, 0.0)
     square_part[...] = jnp.dot(own_rows[...], onehot, precision=HIGHEST, preferred_element_type=f32)
+
+    enter(partner, axes)
+    x, y, z = axes["x"][0], axes["y"][0], axes["z"][0]
+    send(square_part.at[pl.ds(aligned((1 - core) * half_rows, 8), half_rows)], half_rx, 0, 0, partner)
+    panel_piece = count // 4
+    scatter("x", own_rows, 0, panel_piece, panel_rx, 1, 0)
     loads[0].wait()
     weight_part[...] = jnp.dot(weight_ref[...], onehot.astype(bf16), preferred_element_type=f32).astype(bf16)
-
-    enter(partner, axes)
-    x, y, z = axes["x"][0], axes["y"][0], axes["z"][0]
-    s1 = send(square_part.at[pl.ds(aligned((1 - core) * half_rows, 8), half_rows)], half_rx, 0, 0, partner)
-    w1 = send(weight_part.at[pl.ds(aligned((1 - core) * share, 16), share)], weight_rx, 2, 0, partner)
-    panel_piece = count // 4
-    p1 = scatter("x", own_rows, 0, panel_piece, panel_rx, 1)
+    send(weight_part.at[pl.ds(aligned((1 - core) * share, 16), share)], weight_rx, 2, 1, partner)
+    arrive(half_rx, 0)
+    half[...] = square_part[pl.ds(aligned(core * half_rows, 8), half_rows), :] + half_rx[...]
+    scatter("z", half, 0, quarter, z_rx, 3, 0)
     loads[1].wait()
-    features_copy = send(features_ref, features_rx, 18, 0, partner)
-    s1.wait_recv()
-    half[...] = square_part[pl.ds(aligned(core * half_rows, 8), half_rows), :] + half_rx[...]
-    s2 = scatter("z", half, 0, quarter, z_rx, 3)
-    w1.wait_recv()
+    send(features_ref, features_rx, 18, 2, partner)
+    arrive(weight_rx, 2)
     weight_half[...] = weight_part[pl.ds(aligned(core * share, 16), share), :] + weight_rx[...]
     span = share // 2
     piece = span // 4
     small = piece // 4
-    wa = scatter("y", weight_half, 0, piece, first_rx.at[0], 6)
-    wb = scatter("z", weight_half, span, piece, first_rx.at[1], 7)
+    scatter("y", weight_half, 0, piece, first_rx.at[0], 6, 1)
+    scatter("z", weight_half, span, piece, first_rx.at[1], 7, 1)
 
     loads[2].wait()
     limits[...] = jnp.broadcast_to(limit_ref[0:1, :].astype(f32), limits.shape).astype(bf16)
@@ -263,69 +275,68 @@
             )
             kept[spots, :] = jnp.where(seen <= limit, bit, 0.0).astype(bf16)
 
-    arrive(s2)
+    arrive(z_rx, 3)
     z_sum[...] = total(half[pl.ds(aligned(z * quarter, 8), quarter), :], z_rx)
-    s3 = spread("y", z_sum, lambda slot: y_rx.at[slot], 4)
+    spread("y", z_sum, lambda slot: y_rx.at[slot], 4, 0)
     keep(0, chunks)
-    arrive(s3)
+    arrive(y_rx, 4)
     y_sum[...] = total(z_sum[...], y_rx)
-    s4 = spread("x", y_sum, lambda slot: x_rx.at[slot], 5)
-    arrive(wa)
+    spread("x", y_sum, lambda slot: x_rx.at[slot], 5, 0)
+    arrive(first_rx.at[0], 6)
     first_sum[0] = total(weight_half[pl.ds(aligned(y * piece, 16), piece), :], first_rx.at[0])
-    wa = scatter("z", first_sum.at[0], 0, small, second_rx.at[0], 11)
-    arrive(wb)
+    scatter("z", first_sum.at[0], 0, small, second_rx.at[0], 11, 1)
+    arrive(first_rx.at[1], 7)
     first_sum[1] = total(weight_half[pl.ds(aligned(span + z * piece, 16), piece), :], first_rx.at[1])
-    wb = scatter("y", first_sum.at[1], 0, small, second_rx.at[1], 12)
-    arrive(s4)
+    scatter("y", first_sum.at[1], 0, small, second_rx.at[1], 12, 1)
+    arrive(x_rx, 5)
     mine = pl.ds(aligned(core * half_rows + z * quarter, 8), quarter)
     square_ref[mine, :] = total(y_sum[...], x_rx)
-    s5 = spread("z", square_ref.at[mine], lambda slot: square_ref.at[mine], 8)
-    arrive(p1)
+    spread("z", square_ref.at[mine], lambda slot: square_ref.at[mine], 8, 0)
+    arrive(panel_rx, 1)
     own_panel = pl.ds(aligned(x * panel_piece, 8), panel_piece)
     panel_ref[own_panel, :] = total(own_rows[own_panel, :], panel_rx)
-    p2 = spread("x", panel_ref.at[own_panel], lambda slot: panel_ref.at[own_panel], 9)
-    arrive(wa)
+    spread("x", panel_ref.at[own_panel], lambda slot: panel_ref.at[own_panel], 9, 0)
+    arrive(second_rx.at[0], 11)
     base_a = core * share + y * piece
     base_b = core * share + span + z * piece
     slice_a = pl.ds(aligned(base_a + z * small, 16), small)
     slice_b = pl.ds(aligned(base_b + y * small, 16), small)
     chosen_ref[slice_a, :] = total(first_sum[0, pl.ds(aligned(z * small, 16), small), :], second_rx.at[0])
-    wa = spread("z", chosen_ref.at[slice_a], lambda slot: chosen_ref.at[slice_a], 13)
-    arrive(wb)
+    spread("z", chosen_ref.at[slice_a], lambda slot: chosen_ref.at[slice_a], 13, 1)
+    arrive(second_rx.at[1], 12)
     chosen_ref[slice_b, :] = total(first_sum[1, pl.ds(aligned(y * small, 16), small), :], second_rx.at[1])
-    wb = spread("y", chosen_ref.at[slice_b], lambda slot: chosen_ref.at[slice_b], 14)
-    arrive(s5)
+    spread("y", chosen_ref.at[slice_b], lambda slot: chosen_ref.at[slice_b], 14, 1)
+    arrive(square_ref.at[pl.ds(0, 3 * quarter)], 8)
     own_half = pl.ds(aligned(core * half_rows, 8), half_rows)
-    s6 = send(square_ref.at[own_half], square_ref.at[own_half], 10, 0, partner)
+    send(square_ref.at[own_half], square_ref.at[own_half], 10, 0, partner)
     keep(chunks, 2 * chunks)
-    arrive(wa)
+    arrive(chosen_ref.at[pl.ds(0, 3 * small)], 13)
     piece_a = pl.ds(aligned(base_a, 16), piece)
-    wa = spread("y", chosen_ref.at[piece_a], lambda slot: chosen_ref.at[piece_a], 15)
-    arrive(wb)
+    spread("y", chosen_ref.at[piece_a], lambda slot: chosen_ref.at[piece_a], 15, 1)
+    arrive(chosen_ref.at[pl.ds(0, 3 * small)], 14)
     piece_b = pl.ds(aligned(base_b, 16), piece)
-    wb = spread("z", chosen_ref.at[piece_b], lambda slot: chosen_ref.at[piece_b], 16)
-    s6.wait_recv()
+    spread("z", chosen_ref.at[piece_b], lambda slot: chosen_ref.at[piece_b], 16, 1)
+    arrive(square_ref.at[pl.ds(0, half_rows)], 10)
     own_share = pl.ds(aligned(core * share, 16), share)
-    w6 = remote(chosen_ref.at[own_share], chosen_ref.at[own_share], 17, 0, partner)
 
     def between(t):
         @pl.when(t == 1)
         def _():
-            arrive(wa)
-            arrive(wb)
-            w6.start()
+            arrive(chosen_ref.at[pl.ds(0, 3 * piece)], 15)
+            arrive(chosen_ref.at[pl.ds(0, 3 * piece)], 16)
+            send(chosen_ref.at[own_share], chosen_ref.at[own_share], 17, 1, partner)
 
     state[...] = square_ref[...]
     invert(state, right, between)
-    arrive(p2)
+    arrive(panel_ref.at[pl.ds(0, 3 * panel_piece)], 9)
     coeffs = jnp.dot(state[:, :count], panel_ref[...], precision=HIGHEST, preferred_element_type=f32)
     high[...] = coeffs.astype(bf16)
     low[...] = (coeffs - high[...].astype(f32)).astype(bf16)
-    w6.wait_recv()
+    arrive(chosen_ref.at[pl.ds(0, share)], 17)
 
     def pruned_copy(i):
         spots = pl.ds(aligned(i * chunk, chunk), chunk)
-        return pltpu.make_async_copy(pruned_ref.at[spots], pruned_any.at[spots], pruned_sem.at[i])
+        return pltpu.make_async_copy(pruned_ref.at[spots], pruned_any.at[spots], pruned_sem)
 
     def differ(index):
         spots = pl.ds(aligned(index * chunk, chunk), chunk)
@@ -337,12 +348,10 @@
         pruned_ref[spots, :] = masked.astype(bf16)
         return (wide - masked).astype(bf16)
 
-    diff_copies = {}
-
     def prepare(k):
         spots = slice(k * chunk, (k + 1) * chunk)
         sent_diff[spots, :] = differ((1 - core) * chunks + k)
-        diff_copies[k] = send(sent_diff.at[spots], diff_rx.at[spots], 19, k, partner)
+        send(sent_diff.at[spots], diff_rx.at[spots], 20 + k, 2, partner)
         own_diff[spots, :] = differ(core * chunks + k)
 
     token_blocks = part.shape[1]
@@ -362,27 +371,25 @@
             )
             part[k, t] = product.astype(bf16).reshape(part.shape[2:])
 
-    def ring(axis, sent, value, extent, through_rx, through, rx, stage):
+    def ring(axis, parcel, value, extent, through_rx, through, rx, first):
         index, device = axes[axis]
         right_one, left_one, across = lax.rem(index + 1, 4), lax.rem(index + 3, 4), lax.rem(index + 2, 4)
         lo, hi = pl.ds(0, extent // 2), pl.ds(extent // 2, extent // 2)
-        a = send(sent(across).at[lo], through_rx.at[0], stage, 0, device(right_one))
-        b = send(sent(across).at[hi], through_rx.at[1], stage, 1, device(left_one))
-        c = send(sent(right_one).at[hi], rx.at[0, hi], stage, 2, device(right_one))
-        d = send(sent(left_one).at[lo], rx.at[1, lo], stage, 3, device(left_one))
-        later = []
+        send(parcel(across).at[lo], through_rx.at[0], first, 3, device(right_one))
+        send(parcel(across).at[hi], through_rx.at[1], first + 1, 3, device(left_one))
+        send(parcel(right_one).at[hi], rx.at[0, hi], first + 2, 3, device(right_one))
+        send(parcel(left_one).at[lo], rx.at[1, lo], first + 2, 3, device(left_one))
 
         def pass_on():
-            a.wait_recv()
+            arrive(through_rx.at[0], first)
             through[0] = (value(right_one, lo) + through_rx[0].astype(f32)).astype(bf16)
-            later.append(send(through.at[0], rx.at[0, lo], stage, 4, device(right_one)))
-            b.wait_recv()
+            send(through.at[0], rx.at[0, lo], first + 2, 3, device(right_one))
+            arrive(through_rx.at[1], first + 1)
             through[1] = (value(left_one, hi) + through_rx[1].astype(f32)).astype(bf16)
-            later.append(send(through.at[1], rx.at[1, hi], stage, 5, device(left_one)))
+            send(through.at[1], rx.at[1, hi], first + 2, 3, device(left_one))
 
         def finish():
-            for copy in (c, d, *later):
-                copy.wait_recv()
+            arrive(rx, first + 2)
             return value(index, pl.ds(0, extent)) + rx[0].astype(f32) + rx[1].astype(f32)
 
         return pass_on, finish
@@ -392,17 +399,17 @@
 
     def reduce_first(k):
         if k == order[0]:
-            features_copy.wait_recv()
-        diff_copies[k].wait_recv()
+            arrive(features_rx, 18)
+        arrive(diff_rx.at[k * chunk : (k + 1) * chunk], 20 + k)
         multiply(k)
         if k < chunks // 2:
             axis = "y"
-            sent = functools.partial(lambda k, j: part.at[k, j], k)
+            parcel = functools.partial(lambda k, j: part.at[k, j], k)
         else:
             axis = "z"
-            sent = functools.partial(lambda k, j: part.at[k, :, j], k)
-        value = functools.partial(lambda sent, j, which: sent(j).at[which][...].astype(f32), sent)
-        rings[k] = ring(axis, sent, value, 4, forward_rx.at[k], forward.at[k], ring_rx.at[k], 20 + k)
+            parcel = functools.partial(lambda k, j: part.at[k, :, j], k)
+        value = functools.partial(lambda parcel, j, which: parcel(j).at[which][...].astype(f32), parcel)
+        rings[k] = ring(axis, parcel, value, 4, forward_rx.at[k], forward.at[k], ring_rx.at[k], 24 + 3 * k)
 
     prepare(order[0])
     prepare(order[1])
@@ -420,31 +427,28 @@
         sums_wide[k] = value_sum
         sums[k] = value_sum.astype(bf16)
         axis = "z" if k < chunks // 2 else "y"
-        sent = functools.partial(lambda k, j: sums.at[k, j], k)
+        parcel = functools.partial(lambda k, j: sums.at[k, j], k)
         value = functools.partial(lambda k, j, which: sums_wide[k, j, which, :], k)
         again[k] = ring(
-            axis, sent, value, 64, small_forward_rx.at[k], small_forward.at[k], small_rx.at[k], 20 + chunks + k
+            axis, parcel, value, 64, small_forward_rx.at[k], small_forward.at[k], small_rx.at[k],
+            24 + 3 * (chunks + k),
         )
     for k in order:
         again[k][0]()
     tokens = error_ref.shape[0]
-    last = []
     for k in order:
         final[k] = again[k][1]()
         lanes = pl.ds(aligned(core * share + k * chunk, chunk), chunk)
-        last.append(
-            send(
-                final.at[k, pl.ds(aligned((1 - core) * tokens, tokens), tokens)],
-                error_ref.at[:, lanes], 20 + 2 * chunks, k, partner,
-            )
+        send(
+            final.at[k, pl.ds(aligned((1 - core) * tokens, tokens), tokens)], error_ref.at[:, lanes], 19, 0, partner
         )
         error_ref[:, lanes] = final[k, pl.ds(aligned(core * tokens, tokens), tokens), :]
-    for k in range(2 * chunks):
-        pruned_copy(k).wait()
-    arrive(last)
-    w6.wait_send()
-    for copy in started:
-        copy.wait_send()
+    pltpu.make_async_copy(pruned_ref, pruned_any, pruned_sem).wait()
+    arrive(error_ref.at[:, pl.ds(0, share)], 19)
+    unit_bytes = columns * jnp.dtype(weight_ref.dtype).itemsize
+    for group, size in sent.items():
+        view = weight_ref.at[pl.ds(0, size // unit_bytes)]
+        remote(view, view, 0, group, partner).wait_send()
 
 
 def prune(own_rows, line, limit, weight, mask, features, height):
@@ -459,7 +463,7 @@
     chunk = share // chunks
     vmem = pl.BlockSpec(memory_space=pltpu.VMEM)
     hbm = pl.BlockSpec(memory_space=pl.ANY)
-    stages = 21 + 2 * chunks
+    arrivals = 24 + 6 * chunks
     return pl.pallas_call(
         functools.partial(prune_kernel, height=height),
         out_shape=(
@@ -512,10 +516,10 @@
             pltpu.VMEM((chunks, 2, 32, chunk), bf16),
             pltpu.VMEM((chunks, 2, 64, chunk), bf16),
             pltpu.VMEM((chunks, 64, chunk), f32),
-            pltpu.SemaphoreType.DMA((stages, 6)),
-            pltpu.SemaphoreType.DMA((stages, 6)),
+            pltpu.SemaphoreType.DMA((4,)),
+            pltpu.SemaphoreType.DMA((arrivals,)),
             pltpu.SemaphoreType.DMA((3,)),
-            pltpu.SemaphoreType.DMA((2 * chunks,)),
+            pltpu.SemaphoreType.DMA,
         ],
         compiler_params=pltpu.CompilerParams(
             collective_id=0, has_side_effects=True, vmem_limit_bytes=56 << 20

time: 78.1 us -> 71.4 us (0.914)
  Pallas kernels: 73.8 us -> 66.7 us
    pallas_call x1, Pallas kernels: 7.41 us -> 3.79 us  [gather(): pl.pallas_call(gather_kernel, out_shape=(jax.ShapeDtypeStruct((count, inv...]
    pallas_call x1, Pallas kernels: 66.4 us -> 62.9 us  [prune(): pl.pallas_call(functools.partial(prune_kernel, height=height), out_shape=...]
where the time goes in v6:
time: 71.4 us; the launch traced here: 71.1 us
  Pallas kernels  66.7 us (93%)
  local copies, waits for them, and re-layouts  3.79 us (5%)
    pallas_call x1, Pallas kernels, prune(): pl.pallas_call(functools.partial(prune_kernel, height=height), out_shape=...  62.9 us
    unnamed x4, local copies, waits for them, and re-layouts  3.79 us
    pallas_call x1, Pallas kernels, gather(): pl.pallas_call(gather_kernel, out_shape=(jax.ShapeDtypeStruct((count, inv...  3.79 us

profile of v6, /device:TPU:1, one launch (start us, length us, event | category | flops | bytes accessed | tf_op | source)
XLA Modules:
  0.0 71.1 jit_solution(9511069206317622915)
XLA Ops:
  0.6 3.8 %gather.1 = (f32[192,512]{1,0:T(8,128)}, s32[8,256]{1,0:T(8,128)}) custom-call(s32[1]{0:T(128)} %bitcast.offset_ref, s32[3,64]{1,0:T(4,128)} %values_ref.1, s32[3,64]{1,0:T(4,128)} %values_ref.1, f32[4096,512]{1,0:T(8,128)} %inverse_ref.1), custom_call_target="tpu_custom_call" | custom-call | tf_op jit(solution)/shard_map/gather/pallas_call | solution.py:81
  4.4 62.9 %prune.1 = (bf16[2048,512]{1,0:T(8,128)(2,1)}, f32[32,2048]{1,0:T(8,128)}) custom-call(f32[192,512]{1,0:T(8,128)} %get-tuple-element.6.own_ref, s32[8,256]{1,0:T(8,128)} %get-tuple-element.7.line_ref, s32[1,2048]{1,0:T(1,128)} %bitcast.4, bf16[2048,512]{1,0:T(8,128)(2,1)} %weight_any.1, s32[2048,128]{1,0:T(8,128)} %mask_any.1, bf16[1024,512]{1,0:T(8,128)(2,1)} %features_any.1), custom_call_target="tpu_custom_call" | custom-call | tf_op jit(solution)/shard_map/prune/pallas_call | solution.py:467
  67.3 0.0 copy-start
  67.3 3.1 %copy.10 = bf16[2048,512]{1,0:T(8,128)(2,1)} copy(bf16[2048,512]{1,0:T(8,128)(2,1)} %get-tuple-element.12) | data formatting | bytes 4194304
  70.4 0.0 copy-done
  70.4 0.7 copy.11
Async XLA Ops:
  67.3 3.1 %copy-start = (f32[32,2048]{1,0:T(8,128)S(1)}, f32[32,2048]{1,0:T(8,128)}, u32[]{:S(2)}) copy-start(f32[32,2048]{1,0:T(8,128)} %get-tuple-element.9) | copy-start | bytes 786436

commit v7 on v6

--- a/solution.py
+++ b/solution.py
@@ -25,22 +25,25 @@
     y = col // 8
     partner = (row, col + 1 - 2 * core)
     axes = {
-        "x": (row, lambda j: (j, col)),
-        "y": (y, lambda j: (row, (j * 4 + z) * 2 + core)),
-        "z": (z, lambda j: (row, (y * 4 + j) * 2 + core)),
+        "x": (row, lambda j, k=core: (j, (y * 4 + z) * 2 + k)),
+        "y": (y, lambda j, k=core: (row, (j * 4 + z) * 2 + k)),
+        "z": (z, lambda j, k=core: (row, (y * 4 + j) * 2 + k)),
     }
     return core, partner, axes
 
 
-def enter(partner, axes):
+def enter(core, partner, axes):
     barrier = pltpu.get_barrier_semaphore()
-    pl.semaphore_signal(barrier, inc=1, device_id=partner, device_id_type=MESH)
-    for index, device in axes.values():
+    greeted = [partner]
+    for name, (index, device) in axes.items():
         for step in (1, 2, 3):
-            pl.semaphore_signal(
-                barrier, inc=1, device_id=device(lax.rem(index + step, 4)), device_id_type=MESH
-            )
-    pl.semaphore_wait(barrier, 1 + 3 * len(axes))
+            peer = lax.rem(index + step, 4)
+            greeted.append(device(peer))
+            if name != "x":
+                greeted.append(device(peer, 1 - core))
+    for other in greeted:
+        pl.semaphore_signal(barrier, inc=1, device_id=other, device_id_type=MESH)
+    pl.semaphore_wait(barrier, len(greeted))
 
 
 def gather_kernel(offset_ref, selected_ref, values_ref, inverse_ref, own_ref, line_ref, sem):
@@ -98,8 +101,9 @@
     lane = lax.broadcasted_iota(jnp.int32, (size, BLK), 1)
     line = lax.broadcasted_iota(jnp.int32, (size, BLK), 0)
 
-    def column(tile, k):
-        return jnp.broadcast_to(tile[:, k : k + 1], tile.shape)
+    def column(tile, at):
+        picked = jnp.where(lane == at, tile, 0.0)
+        return jnp.broadcast_to(jnp.sum(picked, axis=1, keepdims=True), tile.shape)
 
     def row(tile, k):
         return jnp.broadcast_to(tile[k : k + 1, :], tile.shape)
@@ -113,11 +117,9 @@
         half = t // 2
         shift = (t - half * 2) * side
         lanes = pl.ds(aligned(half * BLK, BLK), BLK)
-        lines = pl.ds(aligned(t * side, side), side)
-        moved = jnp.where(shift > 0, pltpu.roll(state[lines, lanes], side, 1), state[lines, lanes])
-        groups = [moved[i * size : (i + 1) * size] for i in range(blocks)]
+        groups = [state[pl.ds(aligned(t * side + i * size, size), size), lanes] for i in range(blocks)]
         for b in range(blocks):
-            at = b * size
+            at = shift + b * size
             pivot = [column(groups[b], at + j) for j in range(size)]
             for k in range(size):
                 scale = 1.0 / row(pivot[k], k)
@@ -136,15 +138,15 @@
                 change = fold([column(groups[i], at + j) * rows[j] for j in range(size)])
                 groups[i] = jnp.where(inside, 0.0, groups[i]) - change
             groups[b] = fresh
-        block = jnp.concatenate(groups, axis=0)[:, :side]
+        mine = (lane >= shift) & (lane < shift + side)
+        block = jnp.concatenate([jnp.where(mine, group, 0.0) for group in groups], axis=0)
         own = pl.ds(aligned(shift, side), side)
+        lines = pl.ds(aligned(t * side, side), side)
         wide = lax.broadcasted_iota(jnp.int32, (side, width), 1) - t * side
         unit = jnp.where(wide == lax.broadcasted_iota(jnp.int32, (side, width), 0), 1.0, 0.0)
-        solved = jnp.dot(
-            block, jnp.where((wide >= 0) & (wide < side), unit, state[lines, :]),
-            precision=HIGHEST, preferred_element_type=jnp.float32,
-        )
         right[...] = jnp.zeros(right.shape, jnp.float32)
+        right[own, :] = jnp.where((wide >= 0) & (wide < side), unit, state[lines, :])
+        solved = jnp.dot(block, right[...], precision=HIGHEST, preferred_element_type=jnp.float32)
         right[own, :] = solved
         tall = lax.broadcasted_iota(jnp.int32, (count, BLK), 1)
         strip = jnp.where((tall >= shift) & (tall < shift + side), state[:, lanes], 0.0)
@@ -161,10 +163,10 @@
 def prune_kernel(
     own_ref, line_ref, limit_ref, weight_any, mask_any, features_any, pruned_any, error_ref,
     weight_ref, mask_ref, features_ref, kept, limits,
-    own_rows, square_part, half_rx, half, z_rx, z_sum, y_rx, y_sum, x_rx, square_ref, state, right,
+    own_rows, square_part, z_rx, z_sum, y_rx, y_sum, x_rx, square_ref, state, right,
     panel_rx, panel_ref, weight_part, weight_rx, weight_half, first_rx, first_sum, second_rx, chosen_ref,
     high, low, features_rx, own_diff, sent_diff, diff_rx, pruned_ref, part, forward_rx, forward, ring_rx,
-    sums, sums_wide, small_forward_rx, small_forward, small_rx, final,
+    sums, sums_wide, last_rx,
     send_sem, recv_sem, local_sem, pruned_sem,
     *, height,
 ):
@@ -172,8 +174,7 @@
     rows, columns = weight_ref.shape
     col_offset = lax.axis_index("cols") * columns
     count = own_ref.shape[0]
-    half_rows = count // 2
-    quarter = half_rows // 4
+    quarter = count // 8
     share = rows // 2
     chunks = part.shape[0]
     chunk = share // chunks
@@ -218,6 +219,12 @@
         for step in (1, 2, 3):
             send(src, dst_of(step - 1), arrival, group, device(lax.rem(index + step, 4)))
 
+    def around(index):
+        for step in range(4):
+            for turn in range(2):
+                if step + turn > 0:
+                    yield 2 * step + turn - 1, lax.rem(index + step, 4), lax.rem(core + turn, 2)
+
     def total(own, rx):
         return own + rx[0] + rx[1] + rx[2]
 
@@ -234,19 +241,16 @@
     onehot = jnp.where(lines == line_ref[0:1, :], 1.0, 0.0)
     square_part[...] = jnp.dot(own_rows[...], onehot, precision=HIGHEST, preferred_element_type=f32)
 
-    enter(partner, axes)
+    enter(core, partner, axes)
     x, y, z = axes["x"][0], axes["y"][0], axes["z"][0]
-    send(square_part.at[pl.ds(aligned((1 - core) * half_rows, 8), half_rows)], half_rx, 0, 0, partner)
+    for slot, peer, side in around(axes["z"][0]):
+        lines = pl.ds(aligned((side * 4 + peer) * quarter, 8), quarter)
+        send(square_part.at[lines], z_rx.at[slot], 0, 0, axes["z"][1](peer, side))
     panel_piece = count // 4
     scatter("x", own_rows, 0, panel_piece, panel_rx, 1, 0)
     loads[0].wait()
     weight_part[...] = jnp.dot(weight_ref[...], onehot.astype(bf16), preferred_element_type=f32).astype(bf16)
     send(weight_part.at[pl.ds(aligned((1 - core) * share, 16), share)], weight_rx, 2, 1, partner)
-    arrive(half_rx, 0)
-    half[...] = square_part[pl.ds(aligned(core * half_rows, 8), half_rows), :] + half_rx[...]
-    scatter("z", half, 0, quarter, z_rx, 3, 0)
-    loads[1].wait()
-    send(features_ref, features_rx, 18, 2, partner)
     arrive(weight_rx, 2)
     weight_half[...] = weight_part[pl.ds(aligned(core * share, 16), share), :] + weight_rx[...]
     span = share // 2
@@ -275,8 +279,9 @@
             )
             kept[spots, :] = jnp.where(seen <= limit, bit, 0.0).astype(bf16)
 
-    arrive(z_rx, 3)
-    z_sum[...] = total(half[pl.ds(aligned(z * quarter, 8), quarter), :], z_rx)
+    arrive(z_rx, 0)
+    mine = pl.ds(aligned((core * 4 + z) * quarter, 8), quarter)
+    z_sum[...] = total(square_part[mine, :], z_rx) + total(z_rx[3], z_rx.at[pl.ds(4, 3)])
     spread("y", z_sum, lambda slot: y_rx.at[slot], 4, 0)
     keep(0, chunks)
     arrive(y_rx, 4)
@@ -289,9 +294,9 @@
     first_sum[1] = total(weight_half[pl.ds(aligned(span + z * piece, 16), piece), :], first_rx.at[1])
     scatter("y", first_sum.at[1], 0, small, second_rx.at[1], 12, 1)
     arrive(x_rx, 5)
-    mine = pl.ds(aligned(core * half_rows + z * quarter, 8), quarter)
     square_ref[mine, :] = total(y_sum[...], x_rx)
-    spread("z", square_ref.at[mine], lambda slot: square_ref.at[mine], 8, 0)
+    for slot, peer, side in around(z):
+        send(square_ref.at[mine], square_ref.at[mine], 8, 0, axes["z"][1](peer, side))
     arrive(panel_rx, 1)
     own_panel = pl.ds(aligned(x * panel_piece, 8), panel_piece)
     panel_ref[own_panel, :] = total(own_rows[own_panel, :], panel_rx)
@@ -306,9 +311,8 @@
     arrive(second_rx.at[1], 12)
     chosen_ref[slice_b, :] = total(first_sum[1, pl.ds(aligned(y * small, 16), small), :], second_rx.at[1])
     spread("y", chosen_ref.at[slice_b], lambda slot: chosen_ref.at[slice_b], 14, 1)
-    arrive(square_ref.at[pl.ds(0, 3 * quarter)], 8)
-    own_half = pl.ds(aligned(core * half_rows, 8), half_rows)
-    send(square_ref.at[own_half], square_ref.at[own_half], 10, 0, partner)
+    loads[1].wait()
+    send(features_ref, features_rx, 18, 2, partner)
     keep(chunks, 2 * chunks)
     arrive(chosen_ref.at[pl.ds(0, 3 * small)], 13)
     piece_a = pl.ds(aligned(base_a, 16), piece)
@@ -316,7 +320,7 @@
     arrive(chosen_ref.at[pl.ds(0, 3 * small)], 14)
     piece_b = pl.ds(aligned(base_b, 16), piece)
     spread("z", chosen_ref.at[piece_b], lambda slot: chosen_ref.at[piece_b], 16, 1)
-    arrive(square_ref.at[pl.ds(0, half_rows)], 10)
+    arrive(square_ref.at[pl.ds(0, 7 * quarter)], 8)
     own_share = pl.ds(aligned(core * share, 16), share)
 
     def between(t):
@@ -421,30 +425,26 @@
         pruned_copy(k).start()
     for k in order:
         rings[k][0]()
-    again = {}
+    tokens = error_ref.shape[0]
     for k in order:
         value_sum = rings[k][1]()
         sums_wide[k] = value_sum
         sums[k] = value_sum.astype(bf16)
-        axis = "z" if k < chunks // 2 else "y"
-        parcel = functools.partial(lambda k, j: sums.at[k, j], k)
-        value = functools.partial(lambda k, j, which: sums_wide[k, j, which, :], k)
-        again[k] = ring(
-            axis, parcel, value, 64, small_forward_rx.at[k], small_forward.at[k], small_rx.at[k],
-            24 + 3 * (chunks + k),
-        )
+        index, device = axes["z" if k < chunks // 2 else "y"]
+        for slot, peer, side in around(index):
+            words = pl.ds(aligned(side * tokens, tokens), tokens)
+            send(sums.at[k, peer, words], last_rx.at[k, slot], 24 + 3 * chunks + k, 3, device(peer, side))
     for k in order:
-        again[k][0]()
-    tokens = error_ref.shape[0]
-    for k in order:
-        final[k] = again[k][1]()
-        lanes = pl.ds(aligned(core * share + k * chunk, chunk), chunk)
-        send(
-            final.at[k, pl.ds(aligned((1 - core) * tokens, tokens), tokens)], error_ref.at[:, lanes], 19, 0, partner
-        )
-        error_ref[:, lanes] = final[k, pl.ds(aligned(core * tokens, tokens), tokens), :]
+        index = axes["z" if k < chunks // 2 else "y"][0]
+        arrive(last_rx.at[k], 24 + 3 * chunks + k)
+        here_sum = sums_wide[k, index, pl.ds(aligned(core * tokens, tokens), tokens), :]
+        there_sum = last_rx[k, 0].astype(f32)
+        for step in (1, 2, 3):
+            here_sum += last_rx[k, 2 * step - 1].astype(f32)
+            there_sum += last_rx[k, 2 * step].astype(f32)
+        error_ref[:, pl.ds(aligned(core * share + k * chunk, chunk), chunk)] = here_sum
+        error_ref[:, pl.ds(aligned((1 - core) * share + k * chunk, chunk), chunk)] = there_sum
     pltpu.make_async_copy(pruned_ref, pruned_any, pruned_sem).wait()
-    arrive(error_ref.at[:, pl.ds(0, share)], 19)
     unit_bytes = columns * jnp.dtype(weight_ref.dtype).itemsize
     for group, size in sent.items():
         view = weight_ref.at[pl.ds(0, size // unit_bytes)]
@@ -456,14 +456,14 @@
     rows = weight.shape[0]
     tokens = features.shape[0]
     f32, bf16 = jnp.float32, jnp.bfloat16
-    half, quarter = count // 2, count // 8
+    quarter = count // 8
     share, chunks = rows // 2, 4
     piece = share // 8
     small = piece // 4
     chunk = share // chunks
     vmem = pl.BlockSpec(memory_space=pltpu.VMEM)
     hbm = pl.BlockSpec(memory_space=pl.ANY)
-    arrivals = 24 + 6 * chunks
+    arrivals = 24 + 4 * chunks
     return pl.pallas_call(
         functools.partial(prune_kernel, height=height),
         out_shape=(
@@ -480,9 +480,7 @@
             pltpu.VMEM((16, rows), bf16),
             pltpu.VMEM((count, columns), f32),
             pltpu.VMEM((count, LANES), f32),
-            pltpu.VMEM((half, LANES), f32),
-            pltpu.VMEM((half, LANES), f32),
-            pltpu.VMEM((3, quarter, LANES), f32),
+            pltpu.VMEM((7, quarter, LANES), f32),
             pltpu.VMEM((quarter, LANES), f32),
             pltpu.VMEM((3, quarter, LANES), f32),
             pltpu.VMEM((quarter, LANES), f32),
@@ -512,10 +510,7 @@
             pltpu.VMEM((chunks, 2, 4, 64, chunk), bf16),
             pltpu.VMEM((chunks, 4, 64, chunk), bf16),
             pltpu.VMEM((chunks, 4, 64, chunk), f32),
-            pltpu.VMEM((chunks, 2, 32, chunk), bf16),
-            pltpu.VMEM((chunks, 2, 32, chunk), bf16),
-            pltpu.VMEM((chunks, 2, 64, chunk), bf16),
-            pltpu.VMEM((chunks, 64, chunk), f32),
+            pltpu.VMEM((chunks, 7, tokens // 32, chunk), bf16),
             pltpu.SemaphoreType.DMA((4,)),
             pltpu.SemaphoreType.DMA((arrivals,)),
             pltpu.SemaphoreType.DMA((3,)),

time: 71.4 us -> 66.1 us (0.926)
  Pallas kernels: 66.7 us -> 61.4 us
    pallas_call x1, Pallas kernels: 62.9 us -> 57.6 us  [prune(): pl.pallas_call(functools.partial(prune_kernel, height=height), out_shape=...]
where the time goes in v7:
time: 66.1 us; the launch traced here: 65.8 us
  Pallas kernels  61.4 us (93%)
  local copies, waits for them, and re-layouts  3.79 us (6%)
    pallas_call x1, Pallas kernels, prune(): pl.pallas_call(functools.partial(prune_kernel, height=height), out_shape=...  57.6 us
    pallas_call x1, Pallas kernels, gather(): pl.pallas_call(gather_kernel, out_shape=(jax.ShapeDtypeStruct((count, inv...  3.82 us
    unnamed x4, local copies, waits for them, and re-layouts  3.79 us

profile of v7, /device:TPU:1, one launch (start us, length us, event | category | flops | bytes accessed | tf_op | source)
XLA Modules:
  0.0 65.8 jit_solution(8238676562902117889)
XLA Ops:
  0.6 3.8 %gather.1 = (f32[192,512]{1,0:T(8,128)}, s32[8,256]{1,0:T(8,128)}) custom-call(s32[1]{0:T(128)} %bitcast.offset_ref, s32[3,64]{1,0:T(4,128)} %values_ref.1, s32[3,64]{1,0:T(4,128)} %values_ref.1, f32[4096,512]{1,0:T(8,128)} %inverse_ref.1), custom_call_target="tpu_custom_call" | custom-call | tf_op jit(solution)/shard_map/gather/pallas_call | solution.py:84
  4.5 57.6 %prune.1 = (bf16[2048,512]{1,0:T(8,128)(2,1)}, f32[32,2048]{1,0:T(8,128)}) custom-call(f32[192,512]{1,0:T(8,128)} %get-tuple-element.6.own_ref, s32[8,256]{1,0:T(8,128)} %get-tuple-element.7.line_ref, s32[1,2048]{1,0:T(1,128)} %bitcast.4, bf16[2048,512]{1,0:T(8,128)(2,1)} %weight_any.1, s32[2048,128]{1,0:T(8,128)} %mask_any.1, bf16[1024,512]{1,0:T(8,128)(2,1)} %features_any.1), custom_call_target="tpu_custom_call" | custom-call | tf_op jit(solution)/shard_map/prune/pallas_call | solution.py:467
  62.0 0.0 copy-start
  62.1 3.1 %copy.10 = bf16[2048,512]{1,0:T(8,128)(2,1)} copy(bf16[2048,512]{1,0:T(8,128)(2,1)} %get-tuple-element.12) | data formatting | bytes 4194304
  65.1 0.0 copy-done
  65.1 0.7 %copy.11 = f32[2048,32]{0,1:T(8,128)} copy(f32[2048,32]{0,1:T(8,128)S(1)} %bitcast.3) | data formatting | bytes 524288
Async XLA Ops:
  62.0 3.1 %copy-start = (f32[32,2048]{1,0:T(8,128)S(1)}, f32[32,2048]{1,0:T(8,128)}, u32[]{:S(2)}) copy-start(f32[32,2048]{1,0:T(8,128)} %get-tuple-element.9) | copy-start | bytes 786436

commit v8 on v7

--- a/solution.py
+++ b/solution.py
@@ -161,13 +161,13 @@
 
 
 def prune_kernel(
-    own_ref, line_ref, limit_ref, weight_any, mask_any, features_any, pruned_any, error_ref,
+    own_ref, line_ref, limit_ref, weight_any, mask_any, features_any, pruned_ref, error_ref,
     weight_ref, mask_ref, features_ref, kept, limits,
     own_rows, square_part, z_rx, z_sum, y_rx, y_sum, x_rx, square_ref, state, right,
     panel_rx, panel_ref, weight_part, weight_rx, weight_half, first_rx, first_sum, second_rx, chosen_ref,
-    high, low, features_rx, own_diff, sent_diff, diff_rx, pruned_ref, part, forward_rx, forward, ring_rx,
+    high, low, features_rx, own_diff, sent_diff, diff_rx, part, forward_rx, forward, ring_rx,
     sums, sums_wide, last_rx,
-    send_sem, recv_sem, local_sem, pruned_sem,
+    send_sem, recv_sem, local_sem,
     *, height,
 ):
     core, partner, axes = place()
@@ -338,10 +338,6 @@
     low[...] = (coeffs - high[...].astype(f32)).astype(bf16)
     arrive(chosen_ref.at[pl.ds(0, share)], 17)
 
-    def pruned_copy(i):
-        spots = pl.ds(aligned(i * chunk, chunk), chunk)
-        return pltpu.make_async_copy(pruned_ref.at[spots], pruned_any.at[spots], pruned_sem)
-
     def differ(index):
         spots = pl.ds(aligned(index * chunk, chunk), chunk)
         chosen = chosen_ref[spots, :][:, :count]
@@ -352,11 +348,13 @@
         pruned_ref[spots, :] = masked.astype(bf16)
         return (wide - masked).astype(bf16)
 
-    def prepare(k):
+    def prepare_sent(k):
         spots = slice(k * chunk, (k + 1) * chunk)
         sent_diff[spots, :] = differ((1 - core) * chunks + k)
         send(sent_diff.at[spots], diff_rx.at[spots], 20 + k, 2, partner)
-        own_diff[spots, :] = differ(core * chunks + k)
+
+    def prepare_own(k):
+        own_diff[k * chunk : (k + 1) * chunk, :] = differ(core * chunks + k)
 
     token_blocks = part.shape[1]
 
@@ -415,14 +413,14 @@
         value = functools.partial(lambda parcel, j, which: parcel(j).at[which][...].astype(f32), parcel)
         rings[k] = ring(axis, parcel, value, 4, forward_rx.at[k], forward.at[k], ring_rx.at[k], 24 + 3 * k)
 
-    prepare(order[0])
-    prepare(order[1])
+    for k in order:
+        prepare_sent(k)
+    prepare_own(order[0])
+    prepare_own(order[1])
     for n, k in enumerate(order):
         reduce_first(k)
         if n + 2 < chunks:
-            prepare(order[n + 2])
-    for k in range(2 * chunks):
-        pruned_copy(k).start()
+            prepare_own(order[n + 2])
     for k in order:
         rings[k][0]()
     tokens = error_ref.shape[0]
@@ -444,7 +442,6 @@
             there_sum += last_rx[k, 2 * step].astype(f32)
         error_ref[:, pl.ds(aligned(core * share + k * chunk, chunk), chunk)] = here_sum
         error_ref[:, pl.ds(aligned((1 - core) * share + k * chunk, chunk), chunk)] = there_sum
-    pltpu.make_async_copy(pruned_ref, pruned_any, pruned_sem).wait()
     unit_bytes = columns * jnp.dtype(weight_ref.dtype).itemsize
     for group, size in sent.items():
         view = weight_ref.at[pl.ds(0, size // unit_bytes)]
@@ -462,7 +459,7 @@
     small = piece // 4
     chunk = share // chunks
     vmem = pl.BlockSpec(memory_space=pltpu.VMEM)
-    hbm = pl.BlockSpec(memory_space=pl.ANY)
+    hbm = pl.BlockSpec(memory_space=pltpu.HBM)
     arrivals = 24 + 4 * chunks
     return pl.pallas_call(
         functools.partial(prune_kernel, height=height),
@@ -471,7 +468,7 @@
             jax.ShapeDtypeStruct((tokens // 32, rows), f32),
         ),
         in_specs=[vmem, vmem, vmem, hbm, hbm, hbm],
-        out_specs=(hbm, vmem),
+        out_specs=(vmem, vmem),
         scratch_shapes=[
             pltpu.VMEM((rows, columns), bf16),
             pltpu.VMEM(mask.shape, jnp.int32),
@@ -503,7 +500,6 @@
             pltpu.VMEM((share, columns), bf16),
             pltpu.VMEM((share, columns), bf16),
             pltpu.VMEM((share, columns), bf16),
-            pltpu.VMEM((rows, columns), bf16),
             pltpu.VMEM((chunks, 4, 4, 64, chunk), bf16),
             pltpu.VMEM((chunks, 2, 2, 64, chunk), bf16),
             pltpu.VMEM((chunks, 2, 2, 64, chunk), bf16),
@@ -514,10 +510,9 @@
             pltpu.SemaphoreType.DMA((4,)),
             pltpu.SemaphoreType.DMA((arrivals,)),
             pltpu.SemaphoreType.DMA((3,)),
-            pltpu.SemaphoreType.DMA,
         ],
         compiler_params=pltpu.CompilerParams(
-            collective_id=0, has_side_effects=True, vmem_limit_bytes=56 << 20
+            collective_id=0, has_side_effects=True, vmem_limit_bytes=32 << 20
         ),
         name="prune",
     )(own_rows, line, limit, weight, mask, features)

time: 66.1 us -> 65.6 us (level)
  Pallas kernels: 61.4 us -> 59.7 us
  local copies, waits for them, and re-layouts: 3.79 us -> 4.95 us
    pallas_call x1, Pallas kernels: 57.6 us -> 55.8 us  [prune(): pl.pallas_call(functools.partial(prune_kernel, height=height), out_shape=...]
    unnamed x4 -> x14, local copies, waits for them, and re-layouts: 3.79 us -> 4.95 us
where the time goes in v8:
time: 65.6 us; the launch traced here: 65.3 us
  Pallas kernels  59.7 us (91%)
  local copies, waits for them, and re-layouts  4.95 us (8%)
  between operations  0.71 us (1%)
    pallas_call x1, Pallas kernels, prune(): pl.pallas_call(functools.partial(prune_kernel, height=height), out_shape=...  55.8 us
    unnamed x14, local copies, waits for them, and re-layouts  4.95 us
    pallas_call x1, Pallas kernels, gather(): pl.pallas_call(gather_kernel, out_shape=(jax.ShapeDtypeStruct((count, inv...  3.88 us

profile of v8, /device:TPU:1, one launch (start us, length us, event | category | flops | bytes accessed | tf_op | source)
XLA Modules:
  0.0 65.3 jit_solution(4749999296357281695)
XLA Ops:
  0.6 0.0 copy-start
  0.6 0.0 copy-start.1
  0.7 0.0 copy-start.4
  0.7 3.9 %gather.1 = (f32[192,512]{1,0:T(8,128)}, s32[8,256]{1,0:T(8,128)}) custom-call(s32[1]{0:T(128)} %bitcast.offset_ref, s32[3,64]{1,0:T(4,128)} %values_ref.1, s32[3,64]{1,0:T(4,128)} %values_ref.1, f32[4096,512]{1,0:T(8,128)} %inverse_ref.1), custom_call_target="tpu_custom_call" | custom-call | tf_op jit(solution)/shard_map/gather/pallas_call | solution.py:84
  4.6 0.0 copy-done
  4.6 0.0 copy-done.1
  4.6 0.0 copy-done.4
  4.6 0.0 copy-start.2
  4.6 1.2 %copy-done.2 = bf16[1024,512]{1,0:T(8,128)(2,1)S(1)} copy-done((bf16[1024,512]{1,0:T(8,128)(2,1)S(1)}, bf16[1024,512]{1,0:T(8,128)(2,1)}, u32[]{:S(2)}) %copy-start.2) | copy-done | bytes 1048600
  5.8 0.0 copy-start.3
  5.8 1.0 %copy-done.3 = f32[192,512]{1,0:T(8,128)S(1)} copy-done((f32[192,512]{1,0:T(8,128)S(1)}, f32[192,512]{1,0:T(8,128)}, u32[]{:S(2)}) %copy-start.3) | copy-done | bytes 393240
  6.8 0.0 copy-start.5
  6.8 0.7 %copy-done.5 = s32[8,256]{1,0:T(8,128)S(1)} copy-done((s32[8,256]{1,0:T(8,128)S(1)}, s32[8,256]{1,0:T(8,128)}, u32[]{:S(2)}) %copy-start.5) | copy-done | bytes 8216
  7.5 55.8 %prune.1 = (bf16[2048,512]{1,0:T(8,128)(2,1)S(1)}, f32[32,2048]{1,0:T(8,128)S(1)}) custom-call(f32[192,512]{1,0:T(8,128)S(1)} %copy-done.3, s32[8,256]{1,0:T(8,128)S(1)} %copy-done.5, s32[1,2048]{1,0:T(1,128)S(1)} %bitcast.4, bf16[2048,512]{1,0:T(8,128)(2,1)S(1)} %copy-done, s32[2048,128]{1,0:T(8,128)S(1)} %copy-done.1, bf16[1024,512]{1,0:T(8,128)(2,1)S(1)} %copy-done.2), custom_call_target="tpu_custom_call" | custom-call | tf_op jit(solution)/shard_map/prune/pallas_call | solution.py:464
  63.3 1.3 %copy.10 = bf16[2048,512]{1,0:T(8,128)(2,1)} copy(bf16[2048,512]{1,0:T(8,128)(2,1)S(1)} %get-tuple-element.12) | data formatting | bytes 4194304
  64.6 0.7 %copy.11 = f32[2048,32]{0,1:T(8,128)} copy(f32[2048,32]{0,1:T(8,128)S(1)} %bitcast.3) | data formatting | bytes 524288
Async XLA Ops:
  0.6 3.9 %copy-start = (bf16[2048,512]{1,0:T(8,128)(2,1)S(1)}, bf16[2048,512]{1,0:T(8,128)(2,1)}, u32[]{:S(2)}) copy-start(bf16[2048,512]{1,0:T(8,128)(2,1)} %weight_any.1) | copy-start | bytes 6291460
  0.6 3.9 %copy-start.1 = (s32[2048,128]{1,0:T(8,128)S(1)}, s32[2048,128]{1,0:T(8,128)}, u32[]{:S(2)}) copy-start(s32[2048,128]{1,0:T(8,128)} %mask_any.1) | copy-start | bytes 3145732
  0.7 3.9 %copy-start.4 = (s32[2048]{0:T(1024)S(1)}, s32[2048]{0:T(1024)}, u32[]{:S(2)}) copy-start(s32[2048]{0:T(1024)} %param.10) | copy-start | bytes 24580
  4.6 1.2 %copy-start.2 = (bf16[1024,512]{1,0:T(8,128)(2,1)S(1)}, bf16[1024,512]{1,0:T(8,128)(2,1)}, u32[]{:S(2)}) copy-start(bf16[1024,512]{1,0:T(8,128)(2,1)} %features_any.1) | copy-start | bytes 3145732
  5.8 1.0 %copy-start.3 = (f32[192,512]{1,0:T(8,128)S(1)}, f32[192,512]{1,0:T(8,128)}, u32[]{:S(2)}) copy-start(f32[192,512]{1,0:T(8,128)} %get-tuple-element.6.own_ref) | copy-start | bytes 1179652
  6.8 0.7 %copy-start.5 = (s32[8,256]{1,0:T(8,128)S(1)}, s32[8,256]{1,0:T(8,128)}, u32[]{:S(2)}) copy-start(s32[8,256]{1,0:T(8,128)} %get-tuple-element.7.line_ref) | copy-start | bytes 24580

commit v9 on v8

--- a/solution.py
+++ b/solution.py
@@ -161,13 +161,13 @@
 
 
 def prune_kernel(
-    own_ref, line_ref, limit_ref, weight_any, mask_any, features_any, pruned_ref, error_ref,
-    weight_ref, mask_ref, features_ref, kept, limits,
+    own_ref, line_ref, limit_ref, weight_ref, mask_ref, features_ref, pruned_ref, error_ref,
+    kept, limits,
     own_rows, square_part, z_rx, z_sum, y_rx, y_sum, x_rx, square_ref, state, right,
     panel_rx, panel_ref, weight_part, weight_rx, weight_half, first_rx, first_sum, second_rx, chosen_ref,
     high, low, features_rx, own_diff, sent_diff, diff_rx, part, forward_rx, forward, ring_rx,
     sums, sums_wide, last_rx,
-    send_sem, recv_sem, local_sem,
+    send_sem, recv_sem,
     *, height,
 ):
     core, partner, axes = place()
@@ -180,15 +180,6 @@
     chunk = share // chunks
     blocks = columns // BLK
     f32, bf16 = jnp.float32, jnp.bfloat16
-    loads = [
-        pltpu.make_async_copy(src, dst, local_sem.at[i])
-        for i, (src, dst) in enumerate(
-            ((weight_any, weight_ref), (features_any, features_ref), (mask_any, mask_ref))
-        )
-    ]
-    for load in loads:
-        load.start()
-
     sent = {}
 
     def remote(src, dst, arrival, group, device):
@@ -248,7 +239,6 @@
         send(square_part.at[lines], z_rx.at[slot], 0, 0, axes["z"][1](peer, side))
     panel_piece = count // 4
     scatter("x", own_rows, 0, panel_piece, panel_rx, 1, 0)
-    loads[0].wait()
     weight_part[...] = jnp.dot(weight_ref[...], onehot.astype(bf16), preferred_element_type=f32).astype(bf16)
     send(weight_part.at[pl.ds(aligned((1 - core) * share, 16), share)], weight_rx, 2, 1, partner)
     arrive(weight_rx, 2)
@@ -259,7 +249,6 @@
     scatter("y", weight_half, 0, piece, first_rx.at[0], 6, 1)
     scatter("z", weight_half, span, piece, first_rx.at[1], 7, 1)
 
-    loads[2].wait()
     limits[...] = jnp.broadcast_to(limit_ref[0:1, :].astype(f32), limits.shape).astype(bf16)
     place_line = lax.broadcasted_iota(jnp.int32, (BLK, columns), 0)
     block = lax.axis_index("cols") * blocks + lax.broadcasted_iota(jnp.int32, (BLK, columns), 1) // BLK
@@ -311,7 +300,6 @@
     arrive(second_rx.at[1], 12)
     chosen_ref[slice_b, :] = total(first_sum[1, pl.ds(aligned(y * small, 16), small), :], second_rx.at[1])
     spread("y", chosen_ref.at[slice_b], lambda slot: chosen_ref.at[slice_b], 14, 1)
-    loads[1].wait()
     send(features_ref, features_rx, 18, 2, partner)
     keep(chunks, 2 * chunks)
     arrive(chosen_ref.at[pl.ds(0, 3 * small)], 13)
@@ -459,7 +447,6 @@
     small = piece // 4
     chunk = share // chunks
     vmem = pl.BlockSpec(memory_space=pltpu.VMEM)
-    hbm = pl.BlockSpec(memory_space=pltpu.HBM)
     arrivals = 24 + 4 * chunks
     return pl.pallas_call(
         functools.partial(prune_kernel, height=height),
@@ -467,12 +454,9 @@
             jax.ShapeDtypeStruct((rows, columns), bf16),
             jax.ShapeDtypeStruct((tokens // 32, rows), f32),
         ),
-        in_specs=[vmem, vmem, vmem, hbm, hbm, hbm],
+        in_specs=[vmem] * 6,
         out_specs=(vmem, vmem),
         scratch_shapes=[
-            pltpu.VMEM((rows, columns), bf16),
-            pltpu.VMEM(mask.shape, jnp.int32),
-            pltpu.VMEM(features.shape, bf16),
             pltpu.VMEM((rows, columns), bf16),
             pltpu.VMEM((16, rows), bf16),
             pltpu.VMEM((count, columns), f32),
@@ -509,7 +493,6 @@
             pltpu.VMEM((chunks, 7, tokens // 32, chunk), bf16),
             pltpu.SemaphoreType.DMA((4,)),
             pltpu.SemaphoreType.DMA((arrivals,)),
-            pltpu.SemaphoreType.DMA((3,)),
         ],
         compiler_params=pltpu.CompilerParams(
             collective_id=0, has_side_effects=True, vmem_limit_bytes=32 << 20

time: 65.6 us -> 65.4 us (level)
  no operation moved by 1% of the time
where the time goes in v9:
time: 65.4 us; the launch traced here: 65.2 us
  Pallas kernels  59.5 us (91%)
  local copies, waits for them, and re-layouts  4.95 us (8%)
  between operations  0.71 us (1%)
    pallas_call x1, Pallas kernels, prune(): pl.pallas_call(functools.partial(prune_kernel, height=height), out_shape=...  55.6 us
    unnamed x14, local copies, waits for them, and re-layouts  4.95 us
    pallas_call x1, Pallas kernels, gather(): pl.pallas_call(gather_kernel, out_shape=(jax.ShapeDtypeStruct((count, inv...  3.91 us

profile of v9, /device:TPU:1, one launch (start us, length us, event | category | flops | bytes accessed | tf_op | source)
XLA Modules:
  0.0 65.2 jit_solution(18123969833658243378)
XLA Ops:
  0.6 0.0 copy-start
  0.6 0.0 copy-start.1
  0.7 0.0 copy-start.4
  0.7 3.9 %gather.1 = (f32[192,512]{1,0:T(8,128)}, s32[8,256]{1,0:T(8,128)}) custom-call(s32[1]{0:T(128)} %bitcast.offset_ref, s32[3,64]{1,0:T(4,128)} %values_ref.1, s32[3,64]{1,0:T(4,128)} %values_ref.1, f32[4096,512]{1,0:T(8,128)} %inverse_ref.1), custom_call_target="tpu_custom_call" | custom-call | tf_op jit(solution)/shard_map/gather/pallas_call | solution.py:84
  4.6 0.0 copy-done
  4.6 0.0 copy-done.1
  4.6 0.0 copy-done.4
  4.6 0.0 copy-start.2
  4.6 1.2 %copy-done.2 = bf16[1024,512]{1,0:T(8,128)(2,1)S(1)} copy-done((bf16[1024,512]{1,0:T(8,128)(2,1)S(1)}, bf16[1024,512]{1,0:T(8,128)(2,1)}, u32[]{:S(2)}) %copy-start.2) | copy-done | bytes 1048600
  5.8 0.0 copy-start.3
  5.8 1.0 %copy-done.3 = f32[192,512]{1,0:T(8,128)S(1)} copy-done((f32[192,512]{1,0:T(8,128)S(1)}, f32[192,512]{1,0:T(8,128)}, u32[]{:S(2)}) %copy-start.3) | copy-done | bytes 393240
  6.8 0.0 copy-start.5
  6.8 0.7 %copy-done.5 = s32[8,256]{1,0:T(8,128)S(1)} copy-done((s32[8,256]{1,0:T(8,128)S(1)}, s32[8,256]{1,0:T(8,128)}, u32[]{:S(2)}) %copy-start.5) | copy-done | bytes 8216
  7.5 55.6 %prune.1 = (bf16[2048,512]{1,0:T(8,128)(2,1)S(1)}, f32[32,2048]{1,0:T(8,128)S(1)}) custom-call(f32[192,512]{1,0:T(8,128)S(1)} %copy-done.3, s32[8,256]{1,0:T(8,128)S(1)} %copy-done.5, s32[1,2048]{1,0:T(1,128)S(1)} %bitcast.4, bf16[2048,512]{1,0:T(8,128)(2,1)S(1)} %copy-done, s32[2048,128]{1,0:T(8,128)S(1)} %copy-done.1, bf16[1024,512]{1,0:T(8,128)(2,1)S(1)} %copy-done.2), custom_call_target="tpu_custom_call" | custom-call | tf_op jit(solution)/shard_map/prune/pallas_call | solution.py:451
  63.2 1.3 %copy.10 = bf16[2048,512]{1,0:T(8,128)(2,1)} copy(bf16[2048,512]{1,0:T(8,128)(2,1)S(1)} %get-tuple-element.12) | data formatting | bytes 4194304
  64.5 0.7 %copy.11 = f32[2048,32]{0,1:T(8,128)} copy(f32[2048,32]{0,1:T(8,128)S(1)} %bitcast.3) | data formatting | bytes 524288
Async XLA Ops:
  0.6 3.9 %copy-start = (bf16[2048,512]{1,0:T(8,128)(2,1)S(1)}, bf16[2048,512]{1,0:T(8,128)(2,1)}, u32[]{:S(2)}) copy-start(bf16[2048,512]{1,0:T(8,128)(2,1)} %weight_ref.1) | copy-start | bytes 6291460
  0.6 3.9 %copy-start.1 = (s32[2048,128]{1,0:T(8,128)S(1)}, s32[2048,128]{1,0:T(8,128)}, u32[]{:S(2)}) copy-start(s32[2048,128]{1,0:T(8,128)} %mask_ref.1) | copy-start | bytes 3145732
  0.7 3.9 %copy-start.4 = (s32[2048]{0:T(1024)S(1)}, s32[2048]{0:T(1024)}, u32[]{:S(2)}) copy-start(s32[2048]{0:T(1024)} %param.10) | copy-start | bytes 24580
  4.6 1.2 %copy-start.2 = (bf16[1024,512]{1,0:T(8,128)(2,1)S(1)}, bf16[1024,512]{1,0:T(8,128)(2,1)}, u32[]{:S(2)}) copy-start(bf16[1024,512]{1,0:T(8,128)(2,1)} %features_ref.1) | copy-start | bytes 3145732
  5.8 1.0 %copy-start.3 = (f32[192,512]{1,0:T(8,128)S(1)}, f32[192,512]{1,0:T(8,128)}, u32[]{:S(2)}) copy-start(f32[192,512]{1,0:T(8,128)} %get-tuple-element.6.own_ref) | copy-start | bytes 1179652
  6.8 0.7 %copy-start.5 = (s32[8,256]{1,0:T(8,128)S(1)}, s32[8,256]{1,0:T(8,128)}, u32[]{:S(2)}) copy-start(s32[8,256]{1,0:T(8,128)} %get-tuple-element.7.line_ref) | copy-start | bytes 24580
